TPU v7x, 512 devices: a whole 4x4x16 slice. The times are simulated.
512 devices in a mesh: off: 16 (over z_lo, y), img: 32 (over x, z_hi, core).
Axes of the slice: x: 4, y: 4, z: 16 (z_hi: 4, z_lo: 4; z = z_hi * 4 + z_lo), core: 2. Of those that a mesh axis runs over, the one named last changes fastest.
Arguments:
- traces: bfloat16 [16384, 3072], P(('off', 'img')), may hold values from -6 to 6
- offset_bins: int32 [16384], P(('off', 'img')), may hold values from 0 to 15, as said below
- class_slots: int32 [16384], P(('off', 'img')), may hold values from 0 to 1, as said below
- weights: bfloat16 [16, 16384, 1024], P('off', 'img'), may hold values from -0.1875 to 0.1875
- band_start: int32 [16, 128], P('off', 'img'), may hold values from 0 to 1536
- smoothing: int32 [16, 128], P('off', 'img'), may hold values from 0 to 1
Outputs:
- migrated: bfloat16 [16, 16384, 1536], P('off', 'img')
Inputs may be any that keep to these rules, and one draw needn't show every extreme that they name: `offset_bins`: in each aligned block of 32 traces every class is named by exactly 2 traces. Within each aligned block of 32 traces the pairs (offset_bins, class_slots) are all distinct.
All inputs are finite; a program needn't handle non-finite values.
Results may differ from a plain program's by a relative error of at most 0.005.
Values may be sent and summed in bfloat16 or wider, within the bound.
No kernel may reach another device: no remote copies, remote signals or barrier semaphores. Data moves between devices by JAX's collectives and lax.ppermute only.
A program may use at most 128 MiB of HBM per device.

v0:
```python
import jax
import jax.numpy as jnp
from jax import lax
from jax.sharding import PartitionSpec as P

NT = 1536
CB = 128


def filtered_levels(samples):
    values = samples.astype(jnp.float32)
    edges = [(0, 0)] * (values.ndim - 1)
    padded = jnp.pad(values, edges + [(1, 1)])
    boosted = values - 0.5 * (padded[..., :-2] + padded[..., 2:])
    widened = jnp.pad(boosted, edges + [(2, 2)])
    smoothed = (
        3.0 * boosted
        + 2.0 * (widened[..., 1:-3] + widened[..., 3:-1])
        + widened[..., :-4]
        + widened[..., 4:]
    ) / 9.0
    return jnp.stack([boosted, smoothed]).astype(jnp.bfloat16)


def migrate_rows(summed, shard_rows, weight_rows, band_rows, smooth_rows):
    row_count = shard_rows.shape[1]

    def segment(level_index, offset):
        return lax.dynamic_slice(shard_rows, (level_index, 0, offset), (1, row_count, NT))[0]

    segments = jax.vmap(segment)(smooth_rows, band_rows)
    blocks = band_rows.shape[0]
    columns = weight_rows
    columns = columns.reshape(blocks, CB, row_count)
    update = jnp.einsum("bcr,brt->bct", columns, segments, preferred_element_type=jnp.float32)
    return update.reshape(summed.shape)


def per_device(traces, offset_bins, class_slots, weights, band_start, smoothing):
    tr_count = traces.shape[0]
    per_class = tr_count // lax.axis_size("off")
    targets = offset_bins * per_class + class_slots
    weight_rows = weights[0]
    band_rows = band_start[0]
    smooth_rows = smoothing[0]
    initial = jnp.zeros((weight_rows.shape[0], NT), jnp.float32)
    levels = filtered_levels(traces)
    ordered = jnp.zeros_like(levels).at[:, targets].set(levels)
    regrouped = lax.all_to_all(ordered, "off", split_axis=1, concat_axis=1, tiled=True)
    summed = migrate_rows(
        initial,
        lax.all_gather(regrouped, "img", axis=1, tiled=True),
        weight_rows,
        band_rows,
        smooth_rows,
    )
    return summed.astype(jnp.bfloat16)[None]


def solution(mesh):
    in_specs = (
        P(("off", "img"), None),
        P(("off", "img")),
        P(("off", "img")),
        P("off", "img", None),
        P("off", "img"),
        P("off", "img"),
    )
    out_specs = P("off", "img", None)
    return jax.shard_map(
        per_device, mesh=mesh, in_specs=in_specs, out_specs=out_specs, check_vma=False
    )
```

profile of v0, /device:TPU:1, one launch (start us, length us, event | category | flops | bytes accessed | tf_op | source)
XLA Modules:
  0.0 267.9 jit_solution(2371842476114070729)
XLA Ops:
  6.5 0.0 copy-start
  6.5 0.0 all-gather.2.cloned.1.call-start
  6.5 1.0 convert_element_type.24
  7.6 0.3 convert_bitcast_fusion
  7.9 0.5 fusion.8
  8.4 0.4 copy.10
  8.8 0.7 compare_select_fusion.2
  9.5 0.2 broadcast_in_dim.4
  9.7 1.5 scatter_fusion
  11.2 20.6 %all_to_all.5 = bf16[2,32,3072]{2,0,1:T(2,128)(2,1)} all-to-all(bf16[2,32,3072]{2,0,1:T(2,128)(2,1)S(1)} %scatter_fusion), channel_id=1, replica_groups=mesh['off'=16,'img'=32] {'off'}, dimensions={1} | all-to-all | bytes 786432 | tf_op jit(solution)/shard_map/all_to_all | solution.py:49
  31.9 0.0 all-gather.2.cloned.1.call-update
  31.9 0.7 compare_select_fusion
  32.6 0.1 copy.12
  32.7 180.1 %all-gather.2.cloned.1.call-done = bf16[2,1024,3072]{2,0,1:T(2,128)(2,1)} async-done(((bf16[2,32,3072]{2,0,1:T(2,128)(2,1)}), bf16[2,1024,3072]{2,0,1:T(2,128)(2,1)}) %all-gather.2.cloned.1.call-update) | async-done | bytes 12582928 | tf_op jit(solution)/shard_map/all_gather | solution.py:52
  212.8 12.6 %copy.11 = bf16[2,1024,3072]{2,1,0:T(8,128)(2,1)} copy(bf16[2,1024,3072]{2,0,1:T(2,128)(2,1)} %all-gather.2.cloned.1.call-done) | data formatting | bytes 25165824
  225.4 28.1 %while.1 = (s32[]{:T(128)}, bf16[2,1024,3072]{2,1,0:T(8,128)(2,1)}, s32[4,3]{1,0:T(4,128)S(1)}, bf16[4,1,1024,1536]{3,2,1,0:T(8,128)(2,1)}, s32[]{:T(128)}) while((s32[]{:T(128)}, bf16[2,1024,3072]{2,1,0:T(8,128)(2,1)}, s32[4,3]{1,0:T(4,128)S(1)}, bf16[4,1,1024,1536]{3,2,1,0:T(8,128)(2,1)}, s32[]{:T(128)}) %tuple.23), condition=%wide.while_cond, body=%wide.while_body.sunk | while | flops 2 | bytes 6293097 | solution.py:29
  225.4 0.6 fusion.13
  226.0 6.4 %bitcast_dynamic-update-slice_fusion.2 = bf16[4,1,1024,1536]{3,2,1,0:T(8,128)(2,1)} fusion(bf16[4,1,1024,1536]{3,2,1,0:T(8,128)(2,1)} %get-tuple-element.72, s32[]{:T(128)} %get-tuple-element.69, bf16[2,1024,3072]{2,1,0:T(8,128)(2,1)} %get-tuple-element.75, s32[]{:T(128)} %bitcast.28, s32[]{:T(128)} %bitcast.29), kind=kLoop, calls=%fused_computation.1.clone.1 | loop fusion | bytes 6292992 | tf_op jit(solution)/shard_map/vmap()/gather
  232.4 0.6 fusion.13
  233.0 6.4 %bitcast_dynamic-update-slice_fusion.2 = bf16[4,1,1024,1536]{3,2,1,0:T(8,128)(2,1)} fusion(bf16[4,1,1024,1536]{3,2,1,0:T(8,128)(2,1)} %get-tuple-element.72, s32[]{:T(128)} %get-tuple-element.69, bf16[2,1024,3072]{2,1,0:T(8,128)(2,1)} %get-tuple-element.75, s32[]{:T(128)} %bitcast.28, s32[]{:T(128)} %bitcast.29), kind=kLoop, calls=%fused_computation.1.clone.1 | loop fusion | bytes 6292992 | tf_op jit(solution)/shard_map/vmap()/gather
  239.4 0.6 fusion.13
  240.1 6.4 %bitcast_dynamic-update-slice_fusion.2 = bf16[4,1,1024,1536]{3,2,1,0:T(8,128)(2,1)} fusion(bf16[4,1,1024,1536]{3,2,1,0:T(8,128)(2,1)} %get-tuple-element.72, s32[]{:T(128)} %get-tuple-element.69, bf16[2,1024,3072]{2,1,0:T(8,128)(2,1)} %get-tuple-element.75, s32[]{:T(128)} %bitcast.28, s32[]{:T(128)} %bitcast.29), kind=kLoop, calls=%fused_computation.1.clone.1 | loop fusion | bytes 6292992 | tf_op jit(solution)/shard_map/vmap()/gather
  246.5 0.6 fusion.13
  247.1 6.4 %bitcast_dynamic-update-slice_fusion.2 = bf16[4,1,1024,1536]{3,2,1,0:T(8,128)(2,1)} fusion(bf16[4,1,1024,1536]{3,2,1,0:T(8,128)(2,1)} %get-tuple-element.72, s32[]{:T(128)} %get-tuple-element.69, bf16[2,1024,3072]{2,1,0:T(8,128)(2,1)} %get-tuple-element.75, s32[]{:T(128)} %bitcast.28, s32[]{:T(128)} %bitcast.29), kind=kLoop, calls=%fused_computation.1.clone.1 | loop fusion | bytes 6292992 | tf_op jit(solution)/shard_map/vmap()/gather
  253.5 0.0 copy-done
  253.5 7.5 %fusion.2 = bf16[4,1536,128]{1,2,0:T(8,128)(2,1)} fusion(bf16[4,128,1024]{2,1,0:T(8,128)(2,1)S(1)} %bitcast.30, bf16[4,1,1024,1536]{3,2,1,0:T(8,128)(2,1)} %get-tuple-element.12), kind=kOutput, calls=%fused_computation.5 | convolution fusion | flops 1611399168 | bytes 15204352 | tf_op jit(solution)/shard_map/bcr,brt->bct/dot_general | solution.py:35
  (8 shorter events, 0.1 us)
Async XLA Ops:
  6.5 246.9 %copy-start = (bf16[1,512,1024]{2,1,0:T(8,128)(2,1)S(1)}, bf16[1,512,1024]{2,1,0:T(8,128)(2,1)}, u32[]{:S(2)}) copy-start(bf16[1,512,1024]{2,1,0:T(8,128)(2,1)} %param.9) | copy-start | bytes 3145732
  6.5 206.2 %all-gather.2.cloned.1.call-start = ((), (), s32[]{:S(2)}) async-start(), calls=%async_computation.1 | async-start | bytes 12976128 | tf_op jit(solution)/shard_map/all_gather | solution.py:52
Sparse Core Ops, SparseCore 0:
  32.0 180.7 all-gather.1
where the time goes:
time: 268 us
  waiting for transfers between devices  180 us (67%)
  local copies, waits for them, and re-layouts  43 us (16%)
  blocking collectives  20.6 us (8%)
  between operations  13.4 us (5%)
  matrix products  7.54 us (3%)
  other arithmetic  3.2 us (1%)
    all_gather x1, waiting for transfers between devices, per_device(): lax.all_gather(regrouped, 'img', axis=1, tiled=True)  180 us
    gather x12, local copies, waits for them, and re-layouts  28.1 us
    all_to_all x1, blocking collectives, per_device(): lax.all_to_all(ordered, 'off', split_axis=1, concat_axis=1, tiled=True)  20.6 us
    unnamed x4, local copies, waits for them, and re-layouts  12.7 us
    dot_general x1, matrix products, migrate_rows(): jnp.einsum('bcr,brt->bct', columns, segments, preferred_element_type=jnp....  7.54 us
  transfers between devices with their start and end apart: 1, of which 1 were waited for; matrix products, arithmetic and copies ran while one was open for 0% of the time, Pallas kernels for 0%

commit v1 on v0

v1 whole, which is shorter than its diff:
```python
import functools

import jax
import jax.numpy as jnp
from jax import lax
from jax.experimental import pallas as pl
from jax.experimental.pallas import tpu as pltpu
from jax.sharding import Mesh
from jax.sharding import PartitionSpec as P

NT = 1536
NS = 3072
CB = 128
LANES = 128
WINDOW = NT + 3 * LANES
PADDED = NS + 4 * LANES
STEP = 256
ROWS = 16


def ring(axis, count, hop):
    pairs = [(i, (i + hop) % count) for i in range(count)]
    return functools.partial(lax.ppermute, axis_name=axis, perm=pairs)


def lane_shift(values, left):
    width = values.shape[1]
    return pltpu.roll(values, left % width, 1)


def migrate_kernel(
    where_ref, band_ref, level_ref, weights_ref, *refs
):
    pieces, (out_ref, traces, product, sems) = refs[:10], refs[10:]
    me_x, me_c = where_ref[0], where_ref[1]

    copies = []
    for half in range(2):
        core = me_c if half == 0 else 1 - me_c
        own, below, above, far_low, far_high = pieces[5 * half : 5 * half + 5]
        across = lax.rem(me_x + 2, 4)
        places = [
            (own, traces.at[me_x, :, core]),
            (below, traces.at[lax.rem(me_x + 3, 4), :, core]),
            (above, traces.at[lax.rem(me_x + 1, 4), :, core]),
            (far_low, traces.at[across, 0:2, core]),
            (far_high, traces.at[across, 2:4, core]),
        ]
        for source, target in places:
            copy = pltpu.make_async_copy(source, target, sems.at[len(copies)])
            copy.start()
            copies.append(copy)

    rows = product.shape[0]
    product[:, :LANES] = jnp.zeros((rows, LANES), jnp.float32)
    product[:, LANES + NS :] = jnp.zeros((rows, PADDED - NS - LANES), jnp.float32)
    for copy in copies:
        copy.wait()

    def multiply(step, carry):
        at = pl.multiple_of(step * STEP, STEP)
        part = traces[:, :, :, :, pl.ds(at, STEP)].reshape(-1, STEP)
        to = pl.multiple_of(at + LANES, LANES)
        product[:, pl.ds(to, STEP)] = jnp.dot(
            weights_ref[...], part, preferred_element_type=jnp.float32
        )
        return carry

    lax.fori_loop(0, NS // STEP, multiply, 0)

    groups = CB // ROWS
    lane = lax.broadcasted_iota(jnp.int32, (ROWS, WINDOW), 1)
    narrow = lax.broadcasted_iota(jnp.int32, (ROWS, LANES), 1)

    def finish(step, carry):
        block = step // groups
        start = band_ref[block]
        level = level_ref[block]
        tile = start // LANES
        fine = start - tile * LANES
        first = pl.multiple_of(tile * LANES, LANES)
        row = pl.multiple_of(step * ROWS, ROWS)
        raw = product[pl.ds(row, ROWS), pl.ds(first, WINDOW)]
        boosted = raw - 0.5 * (lane_shift(raw, 1) + lane_shift(raw, -1))
        time = lane + (first - LANES)
        boosted = jnp.where((time >= 0) & (time < NS), boosted, 0.0)
        box = boosted + (lane_shift(boosted, 1) + lane_shift(boosted, -1))
        wide = box + (lane_shift(box, 1) + lane_shift(box, -1))
        picked = jnp.where(level > 0, wide * (1.0 / 9.0), boosted)
        back = lax.rem(LANES - fine, LANES)
        turned = [
            pltpu.roll(picked[:, k * LANES : (k + 1) * LANES], back, 1)
            for k in range(1, NT // LANES + 2)
        ]
        keep = narrow < LANES - fine
        for k in range(NT // LANES):
            out_ref[pl.ds(row, ROWS), k * LANES : (k + 1) * LANES] = jnp.where(
                keep, turned[k], turned[k + 1]
            ).astype(out_ref.dtype)
        return carry

    lax.fori_loop(0, rows // ROWS, finish, 0)


def migrate(where, band_start, smoothing, weights, pieces):
    rows = weights.shape[0]
    smem = pl.BlockSpec(memory_space=pltpu.SMEM)
    vmem = pl.BlockSpec(memory_space=pltpu.VMEM)
    anywhere = pl.BlockSpec(memory_space=pl.ANY)
    return pl.pallas_call(
        migrate_kernel,
        out_shape=jax.ShapeDtypeStruct((rows, NT), jnp.bfloat16),
        in_specs=[smem, smem, smem, vmem] + [anywhere] * len(pieces),
        out_specs=vmem,
        scratch_shapes=[
            pltpu.VMEM((4, 4, 2, 32, NS), jnp.bfloat16),
            pltpu.VMEM((rows, PADDED), jnp.float32),
            pltpu.SemaphoreType.DMA((len(pieces),)),
        ],
        compiler_params=pltpu.CompilerParams(vmem_limit_bytes=40 << 20),
        cost_estimate=pl.CostEstimate(
            flops=2 * rows * 1024 * NS, bytes_accessed=9 << 20, transcendentals=0
        ),
    )(where, band_start, smoothing, weights, *pieces)


def per_device(traces, offset_bins, class_slots, weights, band_start, smoothing):
    count = traces.shape[0]
    targets = offset_bins * 2 + class_slots
    chosen = targets[None, :] == jnp.arange(count, dtype=jnp.int32)[:, None]
    ordered = jnp.dot(
        chosen.astype(jnp.bfloat16), traces, preferred_element_type=jnp.float32
    ).astype(jnp.bfloat16)
    copies = jnp.broadcast_to(ordered, (4,) + ordered.shape).reshape(-1, NS)
    own = lax.all_to_all(
        copies, ("zh", "zl", "y"), split_axis=0, concat_axis=0, tiled=True
    ).reshape(4, 32, NS)
    up, down, swap = ring("x", 4, 1), ring("x", 4, 3), ring("c", 2, 1)
    below, above = up(own), down(own)
    far_low, far_high = up(below[:2]), down(above[2:])
    mine = [own, below, above, far_low, far_high]
    other = [swap(piece) for piece in mine]
    where = jnp.stack([lax.axis_index("x"), lax.axis_index("c")]).astype(jnp.int32)
    result = migrate(where, band_start[0], smoothing[0], weights[0], mine + other)
    return result[None]


def solution(mesh):
    fine = Mesh(mesh.devices.reshape(4, 4, 4, 4, 2), ("zl", "y", "x", "zh", "c"))
    off, img = ("zl", "y"), ("x", "zh", "c")
    in_specs = (
        P(off + img, None),
        P(off + img),
        P(off + img),
        P(off, img, None),
        P(off, img),
        P(off, img),
    )
    return jax.shard_map(
        per_device, mesh=fine, in_specs=in_specs, out_specs=P(off, img, None), check_vma=False
    )
```

time: 268 us -> 136 us (0.51)
  waiting for transfers between devices: 180 us -> 14.6 us
  local copies, waits for them, and re-layouts: 43 us -> 2.19 us
  blocking collectives: 20.6 us -> 59.8 us
  starting transfers between devices: 0.01 us -> 35.1 us
  Pallas kernels: 0 us -> 22.8 us
  between operations: 13.4 us -> 0.15 us
  matrix products: 7.54 us -> 0.18 us
    all_gather x1 -> x0, waiting for transfers between devices: 180 us -> none  [per_device(): lax.all_gather(regrouped, 'img', axis=1, tiled=True)]
    all_to_all x1, blocking collectives: 20.6 us -> 59.8 us  [per_device(): lax.all_to_all(copies, ('zh', 'zl', 'y'), split_axis=0, concat_axis=0, ti...]
    ppermute x0 -> x9, starting transfers between devices: none -> 35.1 us  [the longest x5 21.5 us: per_device(): other = [swap(piece) for piece in mine]]
    gather x12 -> x0, local copies, waits for them, and re-layouts: 28.1 us -> none
    pallas_call x0 -> x1, Pallas kernels: none -> 22.8 us  [migrate(): pl.pallas_call(migrate_kernel, out_shape=jax.ShapeDtypeStruct((rows, NT),...]
    ppermute x0 -> x9, waiting for transfers between devices: none -> 14.6 us  [the longest x2 9.04 us: per_device(): far_low, far_high = (up(below[:2]), down(above[2:]))]
    unnamed x4 -> x8, local copies, waits for them, and re-layouts: 12.7 us -> 1.48 us
    dot_general x1, matrix products: 7.54 us -> 0.18 us  [per_device(): jnp.dot(chosen.astype(jnp.bfloat16), traces, preferred_element_type=jnp.f...]
  transfers between devices with their start and end apart: 1 -> 9, of which waited for: 1 -> 3; matrix products, arithmetic and copies ran while one was open for 0% -> 0% of each run, Pallas kernels for 0% -> 0%
where the time goes in v1:
time: 136 us
  blocking collectives  59.8 us (44%)
  starting transfers between devices  35.1 us (26%)
  Pallas kernels  22.8 us (17%)
  waiting for transfers between devices  14.6 us (11%)
  local copies, waits for them, and re-layouts  2.19 us (2%)
    all_to_all x1, blocking collectives, per_device(): lax.all_to_all(copies, ('zh', 'zl', 'y'), split_axis=0, concat_axis=0, ti...  59.8 us
    pallas_call x1, Pallas kernels, migrate(): pl.pallas_call(migrate_kernel, out_shape=jax.ShapeDtypeStruct((rows, NT),...  22.8 us
    ppermute x5, starting transfers between devices, per_device(): other = [swap(piece) for piece in mine]  21.5 us
    ppermute x2, waiting for transfers between devices, per_device(): far_low, far_high = (up(below[:2]), down(above[2:]))  9.04 us
    ppermute x2, starting transfers between devices, per_device(): far_low, far_high = (up(below[:2]), down(above[2:]))  7.24 us
    ppermute x2, starting transfers between devices, per_device(): below, above = (up(own), down(own))  6.31 us
    ppermute x2, waiting for transfers between devices, per_device(): below, above = (up(own), down(own))  4.03 us
  transfers between devices with their start and end apart: 9, of which 3 were waited for; matrix products, arithmetic and copies ran while one was open for 0% of the time, Pallas kernels for 0%

profile of v1, /device:TPU:1, one launch (start us, length us, event | category | flops | bytes accessed | tf_op | source)
XLA Modules:
  0.0 135.6 jit_solution(4882375778265598251)
XLA Ops:
  0.0 0.0 copy-start
  0.0 0.7 multiply_add_fusion
  0.7 0.2 copy-done
  1.0 0.2 convolution_convert_fusion
  1.1 0.1 broadcast_in_dim.8
  1.2 0.3 all_to_all.6
  1.5 59.8 %all_to_all.9 = bf16[64,2,3072]{2,1,0:T(2,128)(2,1)S(1)} all-to-all(bf16[64,2,3072]{2,1,0:T(2,128)(2,1)S(1)} %all_to_all.6), channel_id=1, replica_groups=mesh['zl'=4,'y'=4,'x'=4,'zh'=4,'c'=2] {'zh','zl','y'}, dimensions={0} | all-to-all | bytes 1572864 | tf_op jit(solution)/shard_map/all_to_all | solution.py:135
  61.3 0.0 copy-start.2
  61.3 0.0 copy-start.3
  61.3 0.3 reshape.9.refs_0_
  61.6 4.4 %collective-permute-start.1 = (bf16[4,32,3072]{2,1,0:T(8,128)(2,1)S(1)}, bf16[4,32,3072]{2,1,0:T(8,128)(2,1)S(1)}, u32[]{:S(2)}, u32[]{:S(2)}) collective-permute-start(bf16[4,32,3072]{2,1,0:T(8,128)(2,1)S(1)} %reshape.9.refs_0_), channel_id=1, source_target_pairs={{0,24},{8,0},{16,8},{24,16},{1,25},{9,1},{17,9},{25,17},{2,26},{10... | collective-permute-start | bytes 2359304 | tf_op jit(solution)/shard_map/ppermute | solution.py:139
  66.0 1.9 %collective-permute-start = (bf16[4,32,3072]{2,1,0:T(8,128)(2,1)S(1)}, bf16[4,32,3072]{2,1,0:T(8,128)(2,1)S(1)}, u32[]{:S(2)}, u32[]{:S(2)}) collective-permute-start(bf16[4,32,3072]{2,1,0:T(8,128)(2,1)S(1)} %reshape.9.refs_0_), channel_id=1, source_target_pairs={{0,8},{8,16},{16,24},{24,0},{1,9},{9,17},{17,25},{25,1},{2,10},{10... | collective-permute-start | bytes 2359304 | tf_op jit(solution)/shard_map/ppermute | solution.py:139
  67.9 6.5 %collective-permute-start.4 = (bf16[4,32,3072]{2,1,0:T(8,128)(2,1)S(1)}, bf16[4,32,3072]{2,1,0:T(8,128)(2,1)S(1)}, u32[]{:S(2)}, u32[]{:S(2)}) collective-permute-start(bf16[4,32,3072]{2,1,0:T(8,128)(2,1)S(1)} %reshape.9.refs_0_), channel_id=1, source_target_pairs={{0,1},{1,0},{2,3},{3,2},{4,5},{5,4},{6,7},{7,6},{8,9},{9,8},{10,11... | collective-permute-start | bytes 2359304 | tf_op jit(solution)/shard_map/ppermute | solution.py:142
  74.4 4.0 %collective-permute-done.1.refs_2_ = bf16[4,32,3072]{2,1,0:T(8,128)(2,1)S(1)} collective-permute-done((bf16[4,32,3072]{2,1,0:T(8,128)(2,1)S(1)}, bf16[4,32,3072]{2,1,0:T(8,128)(2,1)S(1)}, u32[]{:S(2)}, u32[]{:S(2)}) %collective-permute-start.1) | collective-permute-done | bytes 786464 | tf_op jit(solution)/shard_map/ppermute | solution.py:139
  78.5 5.3 %collective-permute-start.3 = (bf16[2,32,3072]{2,1,0:T(8,128)(2,1)S(1)}, bf16[2,32,3072]{2,1,0:T(8,128)(2,1)}, u32[]{:S(2)}, u32[]{:S(2)}) collective-permute-start(bf16[2,32,3072]{2,1,0:T(8,128)(2,1)S(1)} %slice.9), channel_id=1, source_target_pairs={{0,24},{8,0},{16,8},{24,16},{1,25},{9,1},{17,9},{25,17},{2,26},{10... | collective-permute-start | bytes 1179656 | tf_op jit(solution)/shard_map/ppermute | solution.py:140
  83.8 7.4 %collective-permute-start.6 = (bf16[4,32,3072]{2,1,0:T(8,128)(2,1)S(1)}, bf16[4,32,3072]{2,1,0:T(8,128)(2,1)}, u32[]{:S(2)}, u32[]{:S(2)}) collective-permute-start(bf16[4,32,3072]{2,1,0:T(8,128)(2,1)S(1)} %collective-permute-done.1.refs_2_), channel_id=1, source_target_pairs={{0,1},{1,0},{2,3},{3,2},{4,5},{5,4},{6,7},{7,6},{8,9},{9,8},{10,11... | collective-permute-start | bytes 2359304 | tf_op jit(solution)/shard_map/ppermute | solution.py:142
  91.3 0.0 collective-permute-done.refs_1_
  91.3 1.9 %collective-permute-start.5 = (bf16[4,32,3072]{2,1,0:T(8,128)(2,1)S(1)}, bf16[4,32,3072]{2,1,0:T(8,128)(2,1)}, u32[]{:S(2)}, u32[]{:S(2)}) collective-permute-start(bf16[4,32,3072]{2,1,0:T(8,128)(2,1)S(1)} %collective-permute-done.refs_1_), channel_id=1, source_target_pairs={{0,1},{1,0},{2,3},{3,2},{4,5},{5,4},{6,7},{7,6},{8,9},{9,8},{10,11... | collective-permute-start | bytes 2359304 | tf_op jit(solution)/shard_map/ppermute | solution.py:142
  93.3 1.9 %collective-permute-start.2 = (bf16[2,32,3072]{2,1,0:T(8,128)(2,1)S(1)}, bf16[2,32,3072]{2,1,0:T(8,128)(2,1)}, u32[]{:S(2)}, u32[]{:S(2)}) collective-permute-start(bf16[2,32,3072]{2,1,0:T(8,128)(2,1)S(1)} %slice.8), channel_id=1, source_target_pairs={{0,8},{8,16},{16,24},{24,0},{1,9},{9,17},{17,25},{25,1},{2,10},{10... | collective-permute-start | bytes 1179656 | tf_op jit(solution)/shard_map/ppermute | solution.py:140
  95.2 0.0 collective-permute-done.3.refs_4_
  95.2 2.4 %collective-permute-start.8 = (bf16[2,32,3072]{2,1,0:T(8,128)(2,1)}, bf16[2,32,3072]{2,1,0:T(8,128)(2,1)}, u32[]{:S(2)}, u32[]{:S(2)}) collective-permute-start(bf16[2,32,3072]{2,1,0:T(8,128)(2,1)} %collective-permute-done.3.refs_4_), channel_id=1, source_target_pairs={{0,1},{1,0},{2,3},{3,2},{4,5},{5,4},{6,7},{7,6},{8,9},{9,8},{10,11... | collective-permute-start | bytes 1179656 | tf_op jit(solution)/shard_map/ppermute | solution.py:142
  97.6 9.0 %collective-permute-done.2.refs_3_ = bf16[2,32,3072]{2,1,0:T(8,128)(2,1)} collective-permute-done((bf16[2,32,3072]{2,1,0:T(8,128)(2,1)S(1)}, bf16[2,32,3072]{2,1,0:T(8,128)(2,1)}, u32[]{:S(2)}, u32[]{:S(2)}) %collective-permute-start.2) | collective-permute-done | bytes 393248 | tf_op jit(solution)/shard_map/ppermute | solution.py:140
  106.7 3.2 %collective-permute-start.7 = (bf16[2,32,3072]{2,1,0:T(8,128)(2,1)}, bf16[2,32,3072]{2,1,0:T(8,128)(2,1)}, u32[]{:S(2)}, u32[]{:S(2)}) collective-permute-start(bf16[2,32,3072]{2,1,0:T(8,128)(2,1)} %collective-permute-done.2.refs_3_), channel_id=1, source_target_pairs={{0,1},{1,0},{2,3},{3,2},{4,5},{5,4},{6,7},{7,6},{8,9},{9,8},{10,11... | collective-permute-start | bytes 1179656 | tf_op jit(solution)/shard_map/ppermute | solution.py:142
  109.9 0.1 pad_add_fusion.where_ref
  110.0 0.0 collective-permute-done.4.refs_5_
  110.0 0.0 collective-permute-done.6.refs_7_
  110.0 0.0 collective-permute-done.5.refs_6_
  110.0 0.0 collective-permute-done.8.refs_9_
  110.0 1.6 %collective-permute-done.7.refs_8_ = bf16[2,32,3072]{2,1,0:T(8,128)(2,1)} collective-permute-done((bf16[2,32,3072]{2,1,0:T(8,128)(2,1)}, bf16[2,32,3072]{2,1,0:T(8,128)(2,1)}, u32[]{:S(2)}, u32[]{:S(2)}) %collective-permute-start.7) | collective-permute-done | bytes 393248 | tf_op jit(solution)/shard_map/ppermute | solution.py:142
  111.6 0.0 copy-done.2
  111.6 0.0 copy-done.3
  111.6 0.0 copy-start.1
  111.6 1.2 copy-done.1
  112.8 22.8 %shard_map.64 = bf16[512,1536]{1,0:T(8,128)(2,1)} custom-call(s32[2]{0:T(128)S(1)} %pad_add_fusion.where_ref, s32[4]{0:T(128)S(1)} %bitcast.8, s32[4]{0:T(128)S(1)} %bitcast.9, bf16[512,1024]{1,0:T(8,128)(2,1)S(1)} %bitcast.7, bf16[4,32,3072]{2,1,0:T(8,128)(2,1)S(1)} %reshape.9.refs_0_, bf16[4,32,3072]{2,1,0:T(8,128)(2,1)S(1)} %collective-permute-done.refs_1_, ...), custom_call_target="tpu_custom_call" | custom-call | flops 3221225472 | bytes 9437184 | tf_op jit(solution)/shard_map/pallas_call | solution.py:110
  (2 shorter events, 0.1 us)
Async XLA Ops:
  0.0 1.0 copy-start
  61.3 50.3 %copy-start.2 = (s32[1,4]{1,0:T(1,128)S(1)}, s32[1,4]{1,0:T(1,128)}, u32[]{:S(2)}) copy-start(s32[1,4]{1,0:T(1,128)} %param.10) | copy-start | bytes 52
  61.3 50.3 %copy-start.3 = (s32[1,4]{1,0:T(1,128)S(1)}, s32[1,4]{1,0:T(1,128)}, u32[]{:S(2)}) copy-start(s32[1,4]{1,0:T(1,128)} %param.11) | copy-start | bytes 52
  61.6 16.9 %collective-permute-start.1 = (bf16[4,32,3072]{2,1,0:T(8,128)(2,1)S(1)}, bf16[4,32,3072]{2,1,0:T(8,128)(2,1)S(1)}, u32[]{:S(2)}, u32[]{:S(2)}) collective-permute-start(bf16[4,32,3072]{2,1,0:T(8,128)(2,1)S(1)} %reshape.9.refs_0_), channel_id=1, source_target_pairs={{0,24},{8,0},{16,8},{24,16},{1,25},{9,1},{17,9},{25,17},{2,26},{10... | collective-permute-start | bytes 2359304 | tf_op jit(solution)/shard_map/ppermute | solution.py:139
  66.0 25.3 %collective-permute-start = (bf16[4,32,3072]{2,1,0:T(8,128)(2,1)S(1)}, bf16[4,32,3072]{2,1,0:T(8,128)(2,1)S(1)}, u32[]{:S(2)}, u32[]{:S(2)}) collective-permute-start(bf16[4,32,3072]{2,1,0:T(8,128)(2,1)S(1)} %reshape.9.refs_0_), channel_id=1, source_target_pairs={{0,8},{8,16},{16,24},{24,0},{1,9},{9,17},{17,25},{25,1},{2,10},{10... | collective-permute-start | bytes 2359304 | tf_op jit(solution)/shard_map/ppermute | solution.py:139
  67.9 42.1 %collective-permute-start.4 = (bf16[4,32,3072]{2,1,0:T(8,128)(2,1)S(1)}, bf16[4,32,3072]{2,1,0:T(8,128)(2,1)S(1)}, u32[]{:S(2)}, u32[]{:S(2)}) collective-permute-start(bf16[4,32,3072]{2,1,0:T(8,128)(2,1)S(1)} %reshape.9.refs_0_), channel_id=1, source_target_pairs={{0,1},{1,0},{2,3},{3,2},{4,5},{5,4},{6,7},{7,6},{8,9},{9,8},{10,11... | collective-permute-start | bytes 2359304 | tf_op jit(solution)/shard_map/ppermute | solution.py:142
  78.5 16.7 %collective-permute-start.3 = (bf16[2,32,3072]{2,1,0:T(8,128)(2,1)S(1)}, bf16[2,32,3072]{2,1,0:T(8,128)(2,1)}, u32[]{:S(2)}, u32[]{:S(2)}) collective-permute-start(bf16[2,32,3072]{2,1,0:T(8,128)(2,1)S(1)} %slice.9), channel_id=1, source_target_pairs={{0,24},{8,0},{16,8},{24,16},{1,25},{9,1},{17,9},{25,17},{2,26},{10... | collective-permute-start | bytes 1179656 | tf_op jit(solution)/shard_map/ppermute | solution.py:140
  83.8 26.2 %collective-permute-start.6 = (bf16[4,32,3072]{2,1,0:T(8,128)(2,1)S(1)}, bf16[4,32,3072]{2,1,0:T(8,128)(2,1)}, u32[]{:S(2)}, u32[]{:S(2)}) collective-permute-start(bf16[4,32,3072]{2,1,0:T(8,128)(2,1)S(1)} %collective-permute-done.1.refs_2_), channel_id=1, source_target_pairs={{0,1},{1,0},{2,3},{3,2},{4,5},{5,4},{6,7},{7,6},{8,9},{9,8},{10,11... | collective-permute-start | bytes 2359304 | tf_op jit(solution)/shard_map/ppermute | solution.py:142
  91.3 18.7 %collective-permute-start.5 = (bf16[4,32,3072]{2,1,0:T(8,128)(2,1)S(1)}, bf16[4,32,3072]{2,1,0:T(8,128)(2,1)}, u32[]{:S(2)}, u32[]{:S(2)}) collective-permute-start(bf16[4,32,3072]{2,1,0:T(8,128)(2,1)S(1)} %collective-permute-done.refs_1_), channel_id=1, source_target_pairs={{0,1},{1,0},{2,3},{3,2},{4,5},{5,4},{6,7},{7,6},{8,9},{9,8},{10,11... | collective-permute-start | bytes 2359304 | tf_op jit(solution)/shard_map/ppermute | solution.py:142
  93.3 13.4 %collective-permute-start.2 = (bf16[2,32,3072]{2,1,0:T(8,128)(2,1)S(1)}, bf16[2,32,3072]{2,1,0:T(8,128)(2,1)}, u32[]{:S(2)}, u32[]{:S(2)}) collective-permute-start(bf16[2,32,3072]{2,1,0:T(8,128)(2,1)S(1)} %slice.8), channel_id=1, source_target_pairs={{0,8},{8,16},{16,24},{24,0},{1,9},{9,17},{17,25},{25,1},{2,10},{10... | collective-permute-start | bytes 1179656 | tf_op jit(solution)/shard_map/ppermute | solution.py:140
  95.2 14.8 %collective-permute-start.8 = (bf16[2,32,3072]{2,1,0:T(8,128)(2,1)}, bf16[2,32,3072]{2,1,0:T(8,128)(2,1)}, u32[]{:S(2)}, u32[]{:S(2)}) collective-permute-start(bf16[2,32,3072]{2,1,0:T(8,128)(2,1)} %collective-permute-done.3.refs_4_), channel_id=1, source_target_pairs={{0,1},{1,0},{2,3},{3,2},{4,5},{5,4},{6,7},{7,6},{8,9},{9,8},{10,11... | collective-permute-start | bytes 1179656 | tf_op jit(solution)/shard_map/ppermute | solution.py:142
  106.7 4.9 %collective-permute-start.7 = (bf16[2,32,3072]{2,1,0:T(8,128)(2,1)}, bf16[2,32,3072]{2,1,0:T(8,128)(2,1)}, u32[]{:S(2)}, u32[]{:S(2)}) collective-permute-start(bf16[2,32,3072]{2,1,0:T(8,128)(2,1)} %collective-permute-done.2.refs_3_), channel_id=1, source_target_pairs={{0,1},{1,0},{2,3},{3,2},{4,5},{5,4},{6,7},{7,6},{8,9},{9,8},{10,11... | collective-permute-start | bytes 1179656 | tf_op jit(solution)/shard_map/ppermute | solution.py:142
  111.6 1.2 copy-start.1

commit v2 on v1

v2 whole, which is shorter than its diff:
```python
import functools

import jax
import jax.numpy as jnp
from jax import lax
from jax.experimental import pallas as pl
from jax.experimental.pallas import tpu as pltpu
from jax.sharding import Mesh
from jax.sharding import PartitionSpec as P

NT = 1536
NS = 3072
CB = 128
LANES = 128
PADDED = NS + 4 * LANES
UNIT = 32
HALF = 48


def ring(axis, count, hop):
    pairs = [(i, (i + hop) % count) for i in range(count)]
    return functools.partial(lax.ppermute, axis_name=axis, perm=pairs)


def gather(piece, axes):
    return lax.all_gather(piece, axes, axis=0, tiled=True)


def spread(piece, first, last, target):
    moves = []
    row = first
    while row < last:
        stop = min(last, (row // UNIT + 1) * UNIT)
        block, low = row // UNIT, row % UNIT
        moves.append((piece.at[row - first : stop - first], target(block).at[low : low + stop - row]))
        row = stop
    return moves


def migrate_kernel(where_ref, band_ref, level_ref, weights_ref, early, *refs):
    pieces, (out_ref, traces, *products, sems) = refs[:10], refs[10:]
    me_x, me_z, me_c = where_ref[0], where_ref[1], where_ref[2]

    moves = [(early, traces.at[:, me_z])]
    for half in range(2):
        core = me_c if half == 0 else 1 - me_c
        for slot, hop, first, last in (
            (0, 0, 0, 2 * HALF),
            (1, 3, 0, 2 * HALF),
            (2, 1, 0, 2 * HALF),
            (3, 2, 0, HALF),
            (4, 2, HALF, 2 * HALF),
        ):
            x = lax.rem(me_x + hop, 4)
            moves += spread(
                pieces[5 * half + slot],
                first,
                last,
                lambda block: traces.at[x, lax.rem(me_z + 1 + block, 4), core],
            )
    copies = []
    for at, (source, target) in enumerate(moves):
        copy = pltpu.make_async_copy(source, target, sems.at[at])
        copy.start()
        copies.append(copy)
    for copy in copies:
        copy.wait()

    lane = lax.broadcasted_iota(jnp.int32, (CB, LANES), 1)
    for block, product in enumerate(products):
        rows = slice(block * CB, (block + 1) * CB)
        product[:, LANES : LANES + NS] = jnp.dot(
            weights_ref[rows, :],
            traces[...].reshape(-1, NS),
            preferred_element_type=jnp.float32,
        )
        first = product[:, LANES : 2 * LANES][:, :1]
        last = product[:, NS : NS + LANES][:, LANES - 1 :]
        product[:, :LANES] = jnp.where(
            lane == LANES - 3, -2.0 * first, jnp.where(lane == LANES - 2, -first, 0.0)
        )
        product[:, LANES + NS : 2 * LANES + NS] = jnp.where(
            lane == 1, -last, jnp.where(lane == 2, -2.0 * last, 0.0)
        )
        product[:, 2 * LANES + NS :] = jnp.zeros((CB, 2 * LANES), jnp.float32)

        start = band_ref[block] + LANES
        smooth = level_ref[block] > 0
        reach = jnp.where(smooth, 3, 1)
        scale = jnp.where(smooth, 1.0 / 9.0, 1.0)
        turned, keeps = [], []
        for at in (start, start - reach, start + reach):
            tile = at // LANES
            fine = at - tile * LANES
            wide = product[:, pl.ds(pl.multiple_of(tile * LANES, LANES), NT + LANES)]
            back = lax.rem(LANES - fine, LANES)
            turned.append(
                [
                    pltpu.roll(wide[:, k * LANES : (k + 1) * LANES], back, 1)
                    for k in range(NT // LANES + 1)
                ]
            )
            keeps.append(lane < LANES - fine)
        for k in range(NT // LANES):
            middle, left, right = [
                jnp.where(keep, tiles[k], tiles[k + 1]) for keep, tiles in zip(keeps, turned)
            ]
            out_ref[rows, k * LANES : (k + 1) * LANES] = (
                (middle - 0.5 * (left + right)) * scale
            ).astype(out_ref.dtype)


def migrate(where, band_start, smoothing, weights, early, pieces):
    rows = weights.shape[0]
    smem = pl.BlockSpec(memory_space=pltpu.SMEM)
    vmem = pl.BlockSpec(memory_space=pltpu.VMEM)
    anywhere = pl.BlockSpec(memory_space=pl.ANY)
    return pl.pallas_call(
        migrate_kernel,
        out_shape=jax.ShapeDtypeStruct((rows, NT), jnp.bfloat16),
        in_specs=[smem, smem, smem, vmem, anywhere] + [anywhere] * len(pieces),
        out_specs=vmem,
        scratch_shapes=[pltpu.VMEM((4, 4, 2, UNIT, NS), jnp.bfloat16)]
        + [pltpu.VMEM((CB, PADDED), jnp.float32)] * (rows // CB)
        + [pltpu.SemaphoreType.DMA((32,))],
        compiler_params=pltpu.CompilerParams(vmem_limit_bytes=40 << 20),
        cost_estimate=pl.CostEstimate(
            flops=2 * rows * 1024 * NS, bytes_accessed=9 << 20, transcendentals=0
        ),
    )(where, band_start, smoothing, weights, early, *pieces)


def per_device(traces, offset_bins, class_slots, weights, band_start, smoothing):
    count = traces.shape[0]
    targets = offset_bins * 2 + class_slots
    chosen = targets[None, :] == jnp.arange(count, dtype=jnp.int32)[:, None]
    ordered = jnp.dot(
        chosen.astype(jnp.bfloat16), traces, preferred_element_type=jnp.float32
    ).astype(jnp.bfloat16)
    mine = lax.all_to_all(ordered, ("zl", "y"), split_axis=0, concat_axis=0, tiled=True)
    early = gather(mine, ("x", "c")).reshape(4, 2, UNIT, NS)
    planes = gather(mine, "zh")
    me_x, me_z, me_c = [lax.axis_index(axis) for axis in ("x", "zh", "c")]
    own = jnp.concatenate(
        [
            lax.dynamic_slice_in_dim(planes, lax.rem(me_z + hop, 4) * UNIT, UNIT)
            for hop in (1, 2, 3)
        ]
    )
    up, down, swap = ring("x", 4, 1), ring("x", 4, 3), ring("c", 2, 1)
    below, above = up(own), down(own)
    far_low, far_high = up(below[:HALF]), down(above[HALF:])
    pieces = [own, below, above, far_low, far_high]
    pieces += [swap(piece) for piece in pieces]
    where = jnp.stack([me_x, me_z, me_c]).astype(jnp.int32)
    return migrate(where, band_start[0], smoothing[0], weights[0], early, pieces)[None]


def solution(mesh):
    fine = Mesh(mesh.devices.reshape(4, 4, 4, 4, 2), ("zl", "y", "x", "zh", "c"))
    off, img = ("zl", "y"), ("x", "zh", "c")
    in_specs = (
        P(off + img, None),
        P(off + img),
        P(off + img),
        P(off, img, None),
        P(off, img),
        P(off, img),
    )
    return jax.shard_map(
        per_device, mesh=fine, in_specs=in_specs, out_specs=P(off, img, None), check_vma=False
    )
```

time: 136 us -> 119 us (0.88)
  between operations: 0.15 us -> 13.6 us
  waiting for transfers between devices: 14.6 us -> 1.48 us
  Pallas kernels: 22.8 us -> 11.4 us
  blocking collectives: 59.8 us -> 53.2 us
    all_to_all x1, blocking collectives: 59.8 us -> 17.4 us  [per_device(): lax.all_to_all(ordered, ('zl', 'y'), split_axis=0, concat_axis=0, tiled=T...]
    all_gather x0 -> x1, blocking collectives: none -> 35.8 us  [gather(): return lax.all_gather(piece, axes, axis=0, tiled=True)]
    pallas_call x1, Pallas kernels: 22.8 us -> 11.4 us  [migrate(): pl.pallas_call(migrate_kernel, out_shape=jax.ShapeDtypeStruct((rows, NT),...]
    ppermute x7, waiting for transfers between devices: 10.6 us -> 1.46 us  [the longest x5 1.45 us: per_device(): pieces += [swap(piece) for piece in pieces]]
    ppermute x2, waiting for transfers between devices: 4.03 us -> 0.01 us  [per_device(): below, above = (up(own), down(own))]
  transfers between devices with their start and end apart: 9 -> 10, of which waited for: 3 -> 1; matrix products, arithmetic and copies ran while one was open for 0% -> 0% of each run, Pallas kernels for 0% -> 0%
where the time goes in v2:
time: 119 us
  blocking collectives  53.2 us (45%)
  starting transfers between devices  35.4 us (30%)
  between operations  13.6 us (11%)
  Pallas kernels  11.4 us (10%)
  local copies, waits for them, and re-layouts  2.57 us (2%)
  waiting for transfers between devices  1.48 us (1%)
    all_gather x1, blocking collectives, gather(): return lax.all_gather(piece, axes, axis=0, tiled=True)  35.8 us
    ppermute x5, starting transfers between devices, per_device(): pieces += [swap(piece) for piece in pieces]  21.7 us
    all_to_all x1, blocking collectives, per_device(): lax.all_to_all(ordered, ('zl', 'y'), split_axis=0, concat_axis=0, tiled=T...  17.4 us
    pallas_call x1, Pallas kernels, migrate(): pl.pallas_call(migrate_kernel, out_shape=jax.ShapeDtypeStruct((rows, NT),...  11.4 us
    ppermute x2, starting transfers between devices, per_device(): far_low, far_high = (up(below[:HALF]), down(above[HALF:]))  7.21 us
    ppermute x2, starting transfers between devices, per_device(): below, above = (up(own), down(own))  6.44 us
  transfers between devices with their start and end apart: 10, of which 1 were waited for; matrix products, arithmetic and copies ran while one was open for 0% of the time, Pallas kernels for 0%

profile of v2, /device:TPU:1, one launch (start us, length us, event | category | flops | bytes accessed | tf_op | source)
XLA Modules:
  0.0 118.7 jit_solution(17914103894302273838)
XLA Ops:
  6.5 0.0 copy-start
  6.5 0.0 all-gather.2.cloned.1.call-start
  6.5 0.7 multiply_add_fusion
  7.3 0.2 copy-done
  7.5 0.2 convolution_convert_fusion
  7.7 0.1 all_to_all.8
  7.8 17.4 %all_to_all.12 = bf16[16,2,3072]{2,1,0:T(2,128)(2,1)S(1)} all-to-all(bf16[16,2,3072]{2,1,0:T(2,128)(2,1)S(1)} %all_to_all.8), channel_id=1, replica_groups=mesh['zl'=4,'y'=4,'x'=4,'zh'=4,'c'=2] {'zl','y'}, dimensions={0} | all-to-all | bytes 393216 | tf_op jit(solution)/shard_map/all_to_all | solution.py:140
  25.2 0.8 all_to_all.10
  25.9 0.0 all-gather.2.cloned.1.call-update
  26.0 35.8 %all_gather.7 = bf16[128,3072]{1,0:T(8,128)(2,1)S(1)} all-gather(bf16[32,3072]{1,0:T(8,128)(2,1)} %all_to_all.10), channel_id=1, replica_groups=mesh['zl'=4,'y'=4,'x'=4,'zh'=4,'c'=2] {'zh'}, dimensions={0}, use_global_device_ids=true | all-gather | bytes 983040 | tf_op jit(solution)/shard_map/all_gather | solution.py:26
  61.8 0.0 copy-start.2
  61.8 0.0 copy-start.3
  61.8 0.0 copy-start.4
  61.9 4.5 %collective-permute-start.1 = (bf16[96,3072]{1,0:T(8,128)(2,1)S(1)}, bf16[96,3072]{1,0:T(8,128)(2,1)S(1)}, u32[]{:S(2)}, u32[]{:S(2)}) collective-permute-start(bf16[96,3072]{1,0:T(8,128)(2,1)S(1)} %pad_maximum_fusion.refs_0_), channel_id=1, source_target_pairs={{0,24},{8,0},{16,8},{24,16},{1,25},{9,1},{17,9},{25,17},{2,26},{10... | collective-permute-start | bytes 1769480 | tf_op jit(solution)/shard_map/ppermute | solution.py:151
  66.4 1.9 %collective-permute-start = (bf16[96,3072]{1,0:T(8,128)(2,1)S(1)}, bf16[96,3072]{1,0:T(8,128)(2,1)S(1)}, u32[]{:S(2)}, u32[]{:S(2)}) collective-permute-start(bf16[96,3072]{1,0:T(8,128)(2,1)S(1)} %pad_maximum_fusion.refs_0_), channel_id=1, source_target_pairs={{0,8},{8,16},{16,24},{24,0},{1,9},{9,17},{17,25},{25,1},{2,10},{10... | collective-permute-start | bytes 1769480 | tf_op jit(solution)/shard_map/ppermute | solution.py:151
  68.4 6.4 %collective-permute-start.4 = (bf16[96,3072]{1,0:T(8,128)(2,1)S(1)}, bf16[96,3072]{1,0:T(8,128)(2,1)}, u32[]{:S(2)}, u32[]{:S(2)}) collective-permute-start(bf16[96,3072]{1,0:T(8,128)(2,1)S(1)} %pad_maximum_fusion.refs_0_), channel_id=1, source_target_pairs={{0,1},{1,0},{2,3},{3,2},{4,5},{5,4},{6,7},{7,6},{8,9},{9,8},{10,11... | collective-permute-start | bytes 1769480 | tf_op jit(solution)/shard_map/ppermute | solution.py:154
  74.8 0.0 collective-permute-done.1.refs_2_
  74.8 5.3 %collective-permute-start.3 = (bf16[48,3072]{1,0:T(8,128)(2,1)S(1)}, bf16[48,3072]{1,0:T(8,128)(2,1)S(1)}, u32[]{:S(2)}, u32[]{:S(2)}) collective-permute-start(bf16[48,3072]{1,0:T(8,128)(2,1)S(1)} %slice.9), channel_id=1, source_target_pairs={{0,24},{8,0},{16,8},{24,16},{1,25},{9,1},{17,9},{25,17},{2,26},{10... | collective-permute-start | bytes 884744 | tf_op jit(solution)/shard_map/ppermute | solution.py:152
  80.1 0.0 collective-permute-done.refs_1_
  80.2 1.9 %collective-permute-start.2 = (bf16[48,3072]{1,0:T(8,128)(2,1)S(1)}, bf16[48,3072]{1,0:T(8,128)(2,1)}, u32[]{:S(2)}, u32[]{:S(2)}) collective-permute-start(bf16[48,3072]{1,0:T(8,128)(2,1)S(1)} %slice.8), channel_id=1, source_target_pairs={{0,8},{8,16},{16,24},{24,0},{1,9},{9,17},{17,25},{25,1},{2,10},{10... | collective-permute-start | bytes 884744 | tf_op jit(solution)/shard_map/ppermute | solution.py:152
  82.1 7.4 %collective-permute-start.6 = (bf16[96,3072]{1,0:T(8,128)(2,1)S(1)}, bf16[96,3072]{1,0:T(8,128)(2,1)}, u32[]{:S(2)}, u32[]{:S(2)}) collective-permute-start(bf16[96,3072]{1,0:T(8,128)(2,1)S(1)} %collective-permute-done.1.refs_2_), channel_id=1, source_target_pairs={{0,1},{1,0},{2,3},{3,2},{4,5},{5,4},{6,7},{7,6},{8,9},{9,8},{10,11... | collective-permute-start | bytes 1769480 | tf_op jit(solution)/shard_map/ppermute | solution.py:154
  89.5 1.9 %collective-permute-start.5 = (bf16[96,3072]{1,0:T(8,128)(2,1)S(1)}, bf16[96,3072]{1,0:T(8,128)(2,1)}, u32[]{:S(2)}, u32[]{:S(2)}) collective-permute-start(bf16[96,3072]{1,0:T(8,128)(2,1)S(1)} %collective-permute-done.refs_1_), channel_id=1, source_target_pairs={{0,1},{1,0},{2,3},{3,2},{4,5},{5,4},{6,7},{7,6},{8,9},{9,8},{10,11... | collective-permute-start | bytes 1769480 | tf_op jit(solution)/shard_map/ppermute | solution.py:154
  91.4 0.0 collective-permute-done.3.refs_4_
  91.4 2.4 %collective-permute-start.8 = (bf16[48,3072]{1,0:T(8,128)(2,1)S(1)}, bf16[48,3072]{1,0:T(8,128)(2,1)}, u32[]{:S(2)}, u32[]{:S(2)}) collective-permute-start(bf16[48,3072]{1,0:T(8,128)(2,1)S(1)} %collective-permute-done.3.refs_4_), channel_id=1, source_target_pairs={{0,1},{1,0},{2,3},{3,2},{4,5},{5,4},{6,7},{7,6},{8,9},{9,8},{10,11... | collective-permute-start | bytes 884744 | tf_op jit(solution)/shard_map/ppermute | solution.py:154
  93.8 0.0 collective-permute-done.2.refs_3_
  93.8 3.6 %collective-permute-start.7 = (bf16[48,3072]{1,0:T(8,128)(2,1)}, bf16[48,3072]{1,0:T(8,128)(2,1)}, u32[]{:S(2)}, u32[]{:S(2)}) collective-permute-start(bf16[48,3072]{1,0:T(8,128)(2,1)} %collective-permute-done.2.refs_3_), channel_id=1, source_target_pairs={{0,1},{1,0},{2,3},{3,2},{4,5},{5,4},{6,7},{7,6},{8,9},{9,8},{10,11... | collective-permute-start | bytes 884744 | tf_op jit(solution)/shard_map/ppermute | solution.py:154
  97.5 0.1 pad_add_fusion.where_ref
  97.5 0.0 collective-permute-done.4.refs_5_
  97.5 0.0 collective-permute-done.8.refs_9_
  97.5 1.4 %collective-permute-done.7.refs_8_ = bf16[48,3072]{1,0:T(8,128)(2,1)} collective-permute-done((bf16[48,3072]{1,0:T(8,128)(2,1)}, bf16[48,3072]{1,0:T(8,128)(2,1)}, u32[]{:S(2)}, u32[]{:S(2)}) %collective-permute-start.7) | collective-permute-done | bytes 294944 | tf_op jit(solution)/shard_map/ppermute | solution.py:154
  99.0 0.0 collective-permute-done.6.refs_7_
  99.0 0.0 collective-permute-done.5.refs_6_
  99.0 0.0 all-gather.2.cloned.1.call-done
  99.0 0.0 copy-done.2
  99.0 0.0 copy-done.3
  99.0 0.0 copy-done.4
  99.0 0.0 copy-start.1
  99.0 1.4 %copy-done.1 = bf16[256,3072]{1,0:T(8,128)(2,1)S(1)} copy-done((bf16[256,3072]{1,0:T(8,128)(2,1)S(1)}, bf16[256,3072]{1,0:T(8,128)(2,1)}, u32[]{:S(2)}) %copy-start.1) | copy-done | bytes 1572888
  100.4 11.4 %shard_map.64 = bf16[512,1536]{1,0:T(8,128)(2,1)} custom-call(s32[3]{0:T(128)S(1)} %pad_add_fusion.where_ref, s32[4]{0:T(128)S(1)} %bitcast.11, s32[4]{0:T(128)S(1)} %bitcast.12, bf16[512,1024]{1,0:T(8,128)(2,1)S(1)} %bitcast.10, bf16[4,2,32,3072]{3,2,1,0:T(8,128)(2,1)S(1)} %bitcast.9, bf16[96,3072]{1,0:T(8,128)(2,1)S(1)} %pad_maximum_fusion.refs_0_, ...), custom_call_target="tpu_custom_call" | custom-call | flops 3221225472 | bytes 9437184 | tf_op jit(solution)/shard_map/pallas_call | solution.py:118
  (4 shorter events, 0.1 us)
Async XLA Ops:
  6.5 1.0 copy-start
  6.5 92.5 %all-gather.2.cloned.1.call-start = ((), (), s32[]{:S(2)}) async-start(), calls=%async_computation.1 | async-start | bytes 1769472 | tf_op jit(solution)/shard_map/all_gather | solution.py:26
  61.8 37.2 %copy-start.2 = (bf16[1,512,1024]{2,1,0:T(8,128)(2,1)S(1)}, bf16[1,512,1024]{2,1,0:T(8,128)(2,1)}, u32[]{:S(2)}) copy-start(bf16[1,512,1024]{2,1,0:T(8,128)(2,1)} %param.9) | copy-start | bytes 3145732
  61.8 37.2 %copy-start.3 = (s32[1,4]{1,0:T(1,128)S(1)}, s32[1,4]{1,0:T(1,128)}, u32[]{:S(2)}) copy-start(s32[1,4]{1,0:T(1,128)} %param.10) | copy-start | bytes 52
  61.8 37.2 %copy-start.4 = (s32[1,4]{1,0:T(1,128)S(1)}, s32[1,4]{1,0:T(1,128)}, u32[]{:S(2)}) copy-start(s32[1,4]{1,0:T(1,128)} %param.11) | copy-start | bytes 52
  61.9 12.9 %collective-permute-start.1 = (bf16[96,3072]{1,0:T(8,128)(2,1)S(1)}, bf16[96,3072]{1,0:T(8,128)(2,1)S(1)}, u32[]{:S(2)}, u32[]{:S(2)}) collective-permute-start(bf16[96,3072]{1,0:T(8,128)(2,1)S(1)} %pad_maximum_fusion.refs_0_), channel_id=1, source_target_pairs={{0,24},{8,0},{16,8},{24,16},{1,25},{9,1},{17,9},{25,17},{2,26},{10... | collective-permute-start | bytes 1769480 | tf_op jit(solution)/shard_map/ppermute | solution.py:151
  66.4 13.7 %collective-permute-start = (bf16[96,3072]{1,0:T(8,128)(2,1)S(1)}, bf16[96,3072]{1,0:T(8,128)(2,1)S(1)}, u32[]{:S(2)}, u32[]{:S(2)}) collective-permute-start(bf16[96,3072]{1,0:T(8,128)(2,1)S(1)} %pad_maximum_fusion.refs_0_), channel_id=1, source_target_pairs={{0,8},{8,16},{16,24},{24,0},{1,9},{9,17},{17,25},{25,1},{2,10},{10... | collective-permute-start | bytes 1769480 | tf_op jit(solution)/shard_map/ppermute | solution.py:151
  68.4 29.2 %collective-permute-start.4 = (bf16[96,3072]{1,0:T(8,128)(2,1)S(1)}, bf16[96,3072]{1,0:T(8,128)(2,1)}, u32[]{:S(2)}, u32[]{:S(2)}) collective-permute-start(bf16[96,3072]{1,0:T(8,128)(2,1)S(1)} %pad_maximum_fusion.refs_0_), channel_id=1, source_target_pairs={{0,1},{1,0},{2,3},{3,2},{4,5},{5,4},{6,7},{7,6},{8,9},{9,8},{10,11... | collective-permute-start | bytes 1769480 | tf_op jit(solution)/shard_map/ppermute | solution.py:154
  74.8 16.6 %collective-permute-start.3 = (bf16[48,3072]{1,0:T(8,128)(2,1)S(1)}, bf16[48,3072]{1,0:T(8,128)(2,1)S(1)}, u32[]{:S(2)}, u32[]{:S(2)}) collective-permute-start(bf16[48,3072]{1,0:T(8,128)(2,1)S(1)} %slice.9), channel_id=1, source_target_pairs={{0,24},{8,0},{16,8},{24,16},{1,25},{9,1},{17,9},{25,17},{2,26},{10... | collective-permute-start | bytes 884744 | tf_op jit(solution)/shard_map/ppermute | solution.py:152
  80.2 13.7 %collective-permute-start.2 = (bf16[48,3072]{1,0:T(8,128)(2,1)S(1)}, bf16[48,3072]{1,0:T(8,128)(2,1)}, u32[]{:S(2)}, u32[]{:S(2)}) collective-permute-start(bf16[48,3072]{1,0:T(8,128)(2,1)S(1)} %slice.8), channel_id=1, source_target_pairs={{0,8},{8,16},{16,24},{24,0},{1,9},{9,17},{17,25},{25,1},{2,10},{10... | collective-permute-start | bytes 884744 | tf_op jit(solution)/shard_map/ppermute | solution.py:152
  82.1 16.9 %collective-permute-start.6 = (bf16[96,3072]{1,0:T(8,128)(2,1)S(1)}, bf16[96,3072]{1,0:T(8,128)(2,1)}, u32[]{:S(2)}, u32[]{:S(2)}) collective-permute-start(bf16[96,3072]{1,0:T(8,128)(2,1)S(1)} %collective-permute-done.1.refs_2_), channel_id=1, source_target_pairs={{0,1},{1,0},{2,3},{3,2},{4,5},{5,4},{6,7},{7,6},{8,9},{9,8},{10,11... | collective-permute-start | bytes 1769480 | tf_op jit(solution)/shard_map/ppermute | solution.py:154
  89.5 9.5 %collective-permute-start.5 = (bf16[96,3072]{1,0:T(8,128)(2,1)S(1)}, bf16[96,3072]{1,0:T(8,128)(2,1)}, u32[]{:S(2)}, u32[]{:S(2)}) collective-permute-start(bf16[96,3072]{1,0:T(8,128)(2,1)S(1)} %collective-permute-done.refs_1_), channel_id=1, source_target_pairs={{0,1},{1,0},{2,3},{3,2},{4,5},{5,4},{6,7},{7,6},{8,9},{9,8},{10,11... | collective-permute-start | bytes 1769480 | tf_op jit(solution)/shard_map/ppermute | solution.py:154
  91.4 6.1 %collective-permute-start.8 = (bf16[48,3072]{1,0:T(8,128)(2,1)S(1)}, bf16[48,3072]{1,0:T(8,128)(2,1)}, u32[]{:S(2)}, u32[]{:S(2)}) collective-permute-start(bf16[48,3072]{1,0:T(8,128)(2,1)S(1)} %collective-permute-done.3.refs_4_), channel_id=1, source_target_pairs={{0,1},{1,0},{2,3},{3,2},{4,5},{5,4},{6,7},{7,6},{8,9},{9,8},{10,11... | collective-permute-start | bytes 884744 | tf_op jit(solution)/shard_map/ppermute | solution.py:154
  93.8 5.2 %collective-permute-start.7 = (bf16[48,3072]{1,0:T(8,128)(2,1)}, bf16[48,3072]{1,0:T(8,128)(2,1)}, u32[]{:S(2)}, u32[]{:S(2)}) collective-permute-start(bf16[48,3072]{1,0:T(8,128)(2,1)} %collective-permute-done.2.refs_3_), channel_id=1, source_target_pairs={{0,1},{1,0},{2,3},{3,2},{4,5},{5,4},{6,7},{7,6},{8,9},{9,8},{10,11... | collective-permute-start | bytes 884744 | tf_op jit(solution)/shard_map/ppermute | solution.py:154
  99.0 1.4 %copy-start.1 = (bf16[256,3072]{1,0:T(8,128)(2,1)S(1)}, bf16[256,3072]{1,0:T(8,128)(2,1)}, u32[]{:S(2)}) copy-start(bf16[256,3072]{1,0:T(8,128)(2,1)} %all-gather.2.cloned.1.call-done) | copy-start | bytes 4718596
Sparse Core Ops, SparseCore 0:
  26.1 33.5 all-gather.1

commit v3 on v2

v3 whole, which is shorter than its diff:
```python
import functools

import jax
import jax.numpy as jnp
from jax import lax
from jax.experimental import pallas as pl
from jax.experimental.pallas import tpu as pltpu
from jax.sharding import Mesh
from jax.sharding import PartitionSpec as P

NT = 1536
NS = 3072
CB = 128
LANES = 128
PADDED = NS + 4 * LANES
SPAN = NT + 2 * LANES


def x_ring(sign):
    pairs = []
    for x in range(4):
        for core in range(2):
            hop = sign if core == 0 else -sign
            pairs.append((2 * x + core, 2 * ((x + hop) % 4) + core))
    return functools.partial(lax.ppermute, axis_name=("x", "c"), perm=pairs)


def swap(piece):
    return lax.ppermute(piece, "c", [(0, 1), (1, 0)])


def arranged(weights_ref, x, me_c):
    old = lax.broadcasted_iota(jnp.int32, (2 * LANES, 2 * LANES), 0)
    new = lax.broadcasted_iota(jnp.int32, (2 * LANES, 2 * LANES), 1)
    core = jnp.where(new < LANES, me_c, 1 - me_c)
    source = (new % LANES) // 32 * 64 + core * 32 + new % 32
    chosen = jnp.where(old == source, 1.0, 0.0).astype(jnp.bfloat16)
    columns = pl.ds(pl.multiple_of(x * 2 * LANES, 2 * LANES), 2 * LANES)
    return jnp.dot(
        weights_ref[:, columns], chosen, preferred_element_type=jnp.float32
    ).astype(jnp.bfloat16)


def own_kernel(where_ref, weights_ref, *refs):
    pieces, (out_ref, sorted_ref) = refs[:-2], refs[-2:]
    me_x, me_c = where_ref[0], where_ref[1]
    nearest = me_x + 3 + 2 * me_c
    for slot, x in enumerate((me_x, nearest, nearest + 2, me_x + 2)):
        sorted_ref[:, slot * 2 * LANES : (slot + 1) * 2 * LANES] = arranged(
            weights_ref, lax.rem(x, 4), me_c
        )
    traces = jnp.concatenate([piece[...] for piece in pieces], axis=0)
    out_ref[...] = jnp.dot(
        sorted_ref[:, : 2 * LANES], traces, preferred_element_type=jnp.float32
    )


def near_kernel(weights_ref, product_ref, *refs):
    pieces, out_ref = refs[:-1], refs[-1]
    traces = jnp.concatenate([piece[...] for piece in pieces], axis=0)
    out_ref[...] = product_ref[...] + jnp.dot(
        weights_ref[:, 2 * LANES : 6 * LANES], traces, preferred_element_type=jnp.float32
    )


def far_kernel(band_ref, level_ref, weights_ref, near_ref, mine_ref, theirs_ref, out_ref, *products):
    lane = lax.broadcasted_iota(jnp.int32, (CB, LANES), 1)
    for block, product in enumerate(products):
        rows = slice(block * CB, (block + 1) * CB)
        at = jnp.clip((band_ref[block] - 3 + LANES) // LANES - 1, 0, (NS - SPAN) // LANES)
        span = pl.ds(pl.multiple_of(at * LANES, LANES), SPAN)
        traces = jnp.concatenate([mine_ref[:, span], theirs_ref[:, span]], axis=0)
        product[:, pl.ds(pl.multiple_of((at + 1) * LANES, LANES), SPAN)] = near_ref[
            rows, span
        ] + jnp.dot(
            weights_ref[rows, 6 * LANES :], traces, preferred_element_type=jnp.float32
        )
        first = product[:, LANES : 2 * LANES][:, :1]
        last = product[:, NS : NS + LANES][:, LANES - 1 :]
        product[:, :LANES] = jnp.where(
            lane == LANES - 3, -2.0 * first, jnp.where(lane == LANES - 2, -first, 0.0)
        )
        product[:, LANES + NS : 2 * LANES + NS] = jnp.where(
            lane == 1, -last, jnp.where(lane == 2, -2.0 * last, 0.0)
        )
        product[:, 2 * LANES + NS :] = jnp.zeros((CB, 2 * LANES), jnp.float32)

        start = band_ref[block] + LANES
        smooth = level_ref[block] > 0
        reach = jnp.where(smooth, 3, 1)
        scale = jnp.where(smooth, 1.0 / 9.0, 1.0)
        turned, keeps = [], []
        for at in (start, start - reach, start + reach):
            tile = at // LANES
            fine = at - tile * LANES
            wide = product[:, pl.ds(pl.multiple_of(tile * LANES, LANES), NT + LANES)]
            back = lax.rem(LANES - fine, LANES)
            turned.append(
                [
                    pltpu.roll(wide[:, k * LANES : (k + 1) * LANES], back, 1)
                    for k in range(NT // LANES + 1)
                ]
            )
            keeps.append(lane < LANES - fine)
        for k in range(NT // LANES):
            middle, left, right = [
                jnp.where(keep, tiles[k], tiles[k + 1]) for keep, tiles in zip(keeps, turned)
            ]
            out_ref[rows, k * LANES : (k + 1) * LANES] = (
                (middle - 0.5 * (left + right)) * scale
            ).astype(out_ref.dtype)


SMEM = pl.BlockSpec(memory_space=pltpu.SMEM)
VMEM = pl.BlockSpec(memory_space=pltpu.VMEM)


def kernel_call(body, outs, in_specs, depth, scratch=()):
    return pl.pallas_call(
        body,
        out_shape=outs,
        in_specs=in_specs,
        out_specs=jax.tree.map(lambda _: VMEM, outs),
        scratch_shapes=list(scratch),
        compiler_params=pltpu.CompilerParams(vmem_limit_bytes=16 << 20),
        cost_estimate=pl.CostEstimate(
            flops=4 * depth * NS, bytes_accessed=depth, transcendentals=0
        ),
    )


def per_device(traces, offset_bins, class_slots, weights, band_start, smoothing):
    count = traces.shape[0]
    targets = offset_bins * 2 + class_slots
    chosen = targets[None, :] == jnp.arange(count, dtype=jnp.int32)[:, None]
    ordered = jnp.dot(
        chosen.astype(jnp.bfloat16), traces, preferred_element_type=jnp.float32
    ).astype(jnp.bfloat16)
    mine = lax.all_to_all(ordered, ("zl", "y"), split_axis=0, concat_axis=0, tiled=True)
    own = lax.all_gather(mine, "zh", axis=0, tiled=True)
    forth, back = x_ring(1), x_ring(-1)
    first, second, own_other = forth(own), back(own), swap(own)
    weights = weights[0]
    rows = weights.shape[0]
    where = jnp.stack([lax.axis_index("x"), lax.axis_index("c")]).astype(jnp.int32)
    product = jax.ShapeDtypeStruct((rows, NS), jnp.float32)
    total, weights = kernel_call(
        own_kernel,
        (product, jax.ShapeDtypeStruct(weights.shape, weights.dtype)),
        [SMEM] + [VMEM] * 3,
        256,
    )(where, weights, own, own_other)
    first, total = lax.optimization_barrier((first, total))
    far = forth(first)
    pieces = [first, swap(second), second, swap(first)]
    far, total = lax.optimization_barrier((far, total))
    total = kernel_call(near_kernel, product, [VMEM] * 6, 512)(weights, total, *pieces)
    return kernel_call(
        far_kernel,
        jax.ShapeDtypeStruct((rows, NT), jnp.bfloat16),
        [SMEM] * 2 + [VMEM] * 4,
        256,
        [pltpu.VMEM((CB, PADDED), jnp.float32)] * (rows // CB),
    )(band_start[0], smoothing[0], weights, total, far, swap(far))[None]


def solution(mesh):
    fine = Mesh(mesh.devices.reshape(4, 4, 4, 4, 2), ("zl", "y", "x", "zh", "c"))
    off, img = ("zl", "y"), ("x", "zh", "c")
    in_specs = (
        P(off + img, None),
        P(off + img),
        P(off + img),
        P(off, img, None),
        P(off, img),
        P(off, img),
    )
    return jax.shard_map(
        per_device, mesh=fine, in_specs=in_specs, out_specs=P(off, img, None), check_vma=False
    )
```

time: 119 us -> 105 us (0.88)
  between operations: 13.6 us -> 0.15 us
  waiting for transfers between devices: 1.48 us -> 13.9 us
  starting transfers between devices: 35.4 us -> 25.8 us
  Pallas kernels: 11.4 us -> 9.18 us
    ppermute x9 -> x7, waiting for transfers between devices: 1.46 us -> 13.9 us  [the longest x2 9.29 us: per_device(): first, second, own_other = (forth(own), back(own), swap(own))]
    ppermute x9 -> x7, starting transfers between devices: 35.4 us -> 25.8 us  [the longest x4 14.2 us: swap(): return lax.ppermute(piece, 'c', [(0, 1), (1, 0)])]
    pallas_call x1 -> x3, Pallas kernels: 11.4 us -> 9.18 us  [the longest x1 5.57 us: per_device(): kernel_call(far_kernel, jax.ShapeDtypeStruct((rows, NT), jnp.bfloat16), [...]
  transfers between devices with their start and end apart: 10 -> 7, of which waited for: 1 -> 2; matrix products, arithmetic and copies ran while one was open for 0% -> 0% of each run, Pallas kernels for 0% -> 3%
where the time goes in v3:
time: 105 us
  blocking collectives  53 us (50%)
  starting transfers between devices  25.8 us (25%)
  waiting for transfers between devices  13.9 us (13%)
  Pallas kernels  9.18 us (9%)
  local copies, waits for them, and re-layouts  1.63 us (2%)
    all_gather x1, blocking collectives, per_device(): own = lax.all_gather(mine, 'zh', axis=0, tiled=True)  35.6 us
    all_to_all x1, blocking collectives, per_device(): lax.all_to_all(ordered, ('zl', 'y'), split_axis=0, concat_axis=0, tiled=T...  17.4 us
    ppermute x4, starting transfers between devices, swap(): return lax.ppermute(piece, 'c', [(0, 1), (1, 0)])  14.2 us
    ppermute x2, waiting for transfers between devices, per_device(): first, second, own_other = (forth(own), back(own), swap(own))  9.29 us
    ppermute x2, starting transfers between devices, per_device(): first, second, own_other = (forth(own), back(own), swap(own))  6.29 us
    pallas_call x1, Pallas kernels, per_device(): kernel_call(far_kernel, jax.ShapeDtypeStruct((rows, NT), jnp.bfloat16), [...  5.57 us
    ppermute x1, starting transfers between devices, per_device(): far = forth(first)  5.31 us
    ppermute x1, waiting for transfers between devices, per_device(): far = forth(first)  4.56 us
  transfers between devices with their start and end apart: 7, of which 2 were waited for; matrix products, arithmetic and copies ran while one was open for 0% of the time, Pallas kernels for 3%

profile of v3, /device:TPU:1, one launch (start us, length us, event | category | flops | bytes accessed | tf_op | source)
XLA Modules:
  0.0 104.6 jit_solution(16290231040394571589)
XLA Ops:
  0.0 0.0 copy-start
  0.0 0.7 multiply_add_fusion
  0.7 0.2 copy-done
  1.0 0.2 convolution_convert_fusion
  1.1 0.1 all_to_all.8
  1.2 17.4 %all_to_all.12 = bf16[16,2,3072]{2,1,0:T(2,128)(2,1)S(1)} all-to-all(bf16[16,2,3072]{2,1,0:T(2,128)(2,1)S(1)} %all_to_all.8), channel_id=1, replica_groups=mesh['zl'=4,'y'=4,'x'=4,'zh'=4,'c'=2] {'zl','y'}, dimensions={0} | all-to-all | bytes 393216 | tf_op jit(solution)/shard_map/all_to_all | solution.py:139
  18.6 0.1 all_to_all.10
  18.7 35.6 %all_gather.3.refs_0_ = bf16[128,3072]{1,0:T(8,128)(2,1)S(1)} all-gather(bf16[32,3072]{1,0:T(8,128)(2,1)S(1)} %all_to_all.10), channel_id=1, replica_groups=mesh['zl'=4,'y'=4,'x'=4,'zh'=4,'c'=2] {'zh'}, dimensions={0}, use_global_device_ids=true | all-gather | bytes 983040 | tf_op jit(solution)/shard_map/all_gather | solution.py:140
  54.3 6.1 %collective-permute-start = (bf16[128,3072]{1,0:T(8,128)(2,1)S(1)}, bf16[128,3072]{1,0:T(8,128)(2,1)S(1)}, u32[]{:S(2)}, u32[]{:S(2)}) collective-permute-start(bf16[128,3072]{1,0:T(8,128)(2,1)S(1)} %all_gather.3.refs_0_), channel_id=1, source_target_pairs={{0,1},{1,0},{2,3},{3,2},{4,5},{5,4},{6,7},{7,6},{8,9},{9,8},{10,11... | collective-permute-start | bytes 2359304 | tf_op jit(solution)/shard_map/ppermute | solution.py:29
  60.5 4.4 %collective-permute-start.1 = (bf16[128,3072]{1,0:T(8,128)(2,1)S(1)}, bf16[128,3072]{1,0:T(8,128)(2,1)S(1)}, u32[]{:S(2)}, u32[]{:S(2)}) collective-permute-start(bf16[128,3072]{1,0:T(8,128)(2,1)S(1)} %all_gather.3.refs_0_), channel_id=1, source_target_pairs={{0,8},{1,25},{8,16},{9,1},{16,24},{17,9},{24,0},{25,17},{2,10},{3,... | collective-permute-start | bytes 2359304 | tf_op jit(solution)/shard_map/ppermute | solution.py:142
  64.9 0.1 pad_add_fusion.where_ref
  64.9 1.9 %collective-permute-start.3 = (bf16[128,3072]{1,0:T(8,128)(2,1)S(1)}, bf16[128,3072]{1,0:T(8,128)(2,1)S(1)}, u32[]{:S(2)}, u32[]{:S(2)}) collective-permute-start(bf16[128,3072]{1,0:T(8,128)(2,1)S(1)} %all_gather.3.refs_0_), channel_id=1, source_target_pairs={{0,24},{1,9},{8,0},{9,17},{16,8},{17,25},{24,16},{25,1},{2,26},{3,... | collective-permute-start | bytes 2359304 | tf_op jit(solution)/shard_map/ppermute | solution.py:142
  66.9 0.0 collective-permute-done.refs_1_
  66.9 0.0 copy-start.1
  66.9 1.2 %copy-done.1 = bf16[1,512,1024]{2,1,0:T(8,128)(2,1)S(1)} copy-done((bf16[1,512,1024]{2,1,0:T(8,128)(2,1)S(1)}, bf16[1,512,1024]{2,1,0:T(8,128)(2,1)}, u32[]{:S(2)}) %copy-start.1) | copy-done | bytes 1048600
  68.1 1.8 %shard_map.64 = (f32[512,3072]{1,0:T(8,128)S(1)}, bf16[512,1024]{1,0:T(8,128)(2,1)S(1)}) custom-call(s32[2]{0:T(128)S(1)} %pad_add_fusion.where_ref, bf16[512,1024]{1,0:T(8,128)(2,1)S(1)} %bitcast.7, bf16[128,3072]{1,0:T(8,128)(2,1)S(1)} %all_gather.3.refs_0_, bf16[128,3072]{1,0:T(8,128)(2,1)S(1)} %collective-permute-done.refs_1_), custom_call_target="tpu_custom_call" | custom-call | flops 3145728 | bytes 256 | tf_op jit(solution)/shard_map/pallas_call | solution.py:147
  69.9 9.3 %collective-permute-done.1.refs_0_ = bf16[128,3072]{1,0:T(8,128)(2,1)S(1)} collective-permute-done((bf16[128,3072]{1,0:T(8,128)(2,1)S(1)}, bf16[128,3072]{1,0:T(8,128)(2,1)S(1)}, u32[]{:S(2)}, u32[]{:S(2)}) %collective-permute-start.1) | collective-permute-done | bytes 786464 | tf_op jit(solution)/shard_map/ppermute | solution.py:142
  79.2 5.3 %collective-permute-start.2 = (bf16[128,3072]{1,0:T(8,128)(2,1)S(1)}, bf16[128,3072]{1,0:T(8,128)(2,1)S(1)}, u32[]{:S(2)}, u32[]{:S(2)}) collective-permute-start(bf16[128,3072]{1,0:T(8,128)(2,1)S(1)} %collective-permute-done.1.refs_0_), channel_id=1, source_target_pairs={{0,8},{1,25},{8,16},{9,1},{16,24},{17,9},{24,0},{25,17},{2,10},{3,... | collective-permute-start | bytes 2359304 | tf_op jit(solution)/shard_map/ppermute | solution.py:154
  84.5 0.0 collective-permute-done.3.refs_2_
  84.5 1.9 %collective-permute-start.4 = (bf16[128,3072]{1,0:T(8,128)(2,1)S(1)}, bf16[128,3072]{1,0:T(8,128)(2,1)S(1)}, u32[]{:S(2)}, u32[]{:S(2)}) collective-permute-start(bf16[128,3072]{1,0:T(8,128)(2,1)S(1)} %collective-permute-done.3.refs_2_), channel_id=1, source_target_pairs={{0,1},{1,0},{2,3},{3,2},{4,5},{5,4},{6,7},{7,6},{8,9},{9,8},{10,11... | collective-permute-start | bytes 2359304 | tf_op jit(solution)/shard_map/ppermute | solution.py:29
  86.4 2.4 %collective-permute-start.5 = (bf16[128,3072]{1,0:T(8,128)(2,1)S(1)}, bf16[128,3072]{1,0:T(8,128)(2,1)S(1)}, u32[]{:S(2)}, u32[]{:S(2)}) collective-permute-start(bf16[128,3072]{1,0:T(8,128)(2,1)S(1)} %collective-permute-done.1.refs_0_), channel_id=1, source_target_pairs={{0,1},{1,0},{2,3},{3,2},{4,5},{5,4},{6,7},{7,6},{8,9},{9,8},{10,11... | collective-permute-start | bytes 2359304 | tf_op jit(solution)/shard_map/ppermute | solution.py:29
  88.9 4.6 %collective-permute-done.2.mine_ref = bf16[128,3072]{1,0:T(8,128)(2,1)S(1)} collective-permute-done((bf16[128,3072]{1,0:T(8,128)(2,1)S(1)}, bf16[128,3072]{1,0:T(8,128)(2,1)S(1)}, u32[]{:S(2)}, u32[]{:S(2)}) %collective-permute-start.2) | collective-permute-done | bytes 786464 | tf_op jit(solution)/shard_map/ppermute | solution.py:154
  93.4 3.7 %collective-permute-start.6 = (bf16[128,3072]{1,0:T(8,128)(2,1)S(1)}, bf16[128,3072]{1,0:T(8,128)(2,1)S(1)}, u32[]{:S(2)}, u32[]{:S(2)}) collective-permute-start(bf16[128,3072]{1,0:T(8,128)(2,1)S(1)} %collective-permute-done.2.mine_ref), channel_id=1, source_target_pairs={{0,1},{1,0},{2,3},{3,2},{4,5},{5,4},{6,7},{7,6},{8,9},{9,8},{10,11... | collective-permute-start | bytes 2359304 | tf_op jit(solution)/shard_map/ppermute | solution.py:29
  97.2 0.0 collective-permute-done.4.refs_1_
  97.2 0.0 collective-permute-done.5.refs_3_
  97.2 0.0 copy-start.2
  97.2 0.0 copy-start.3
  97.2 1.8 %shard_map.65.near_ref = f32[512,3072]{1,0:T(8,128)S(1)} custom-call(bf16[512,1024]{1,0:T(8,128)(2,1)S(1)} %get-tuple-element.11.weights_ref, f32[512,3072]{1,0:T(8,128)S(1)} %get-tuple-element.15.product_ref, bf16[128,3072]{1,0:T(8,128)(2,1)S(1)} %collective-permute-done.1.refs_0_, bf16[128,3072]{1,0:T(8,128)(2,1)S(1)} %collective-permute-done.4.refs_1_, ...), custom_call_target="tpu_custom_call" | custom-call | flops 6291456 | bytes 512 | tf_op jit(solution)/shard_map/pallas_call | solution.py:157
  99.0 0.0 collective-permute-done.6.theirs_ref
  99.1 0.0 copy-done.2
  99.1 0.0 copy-done.3
  99.1 5.6 %shard_map.66 = bf16[512,1536]{1,0:T(8,128)(2,1)} custom-call(s32[4]{0:T(128)S(1)} %bitcast.8, s32[4]{0:T(128)S(1)} %bitcast.9, bf16[512,1024]{1,0:T(8,128)(2,1)S(1)} %get-tuple-element.11.weights_ref, f32[512,3072]{1,0:T(8,128)S(1)} %shard_map.65.near_ref, bf16[128,3072]{1,0:T(8,128)(2,1)S(1)} %collective-permute-done.2.mine_ref, ...), custom_call_target="tpu_custom_call" | custom-call | flops 3145728 | bytes 256 | tf_op jit(solution)/shard_map/pallas_call | solution.py:158
Async XLA Ops:
  0.0 1.0 copy-start
  54.3 12.6 %collective-permute-start = (bf16[128,3072]{1,0:T(8,128)(2,1)S(1)}, bf16[128,3072]{1,0:T(8,128)(2,1)S(1)}, u32[]{:S(2)}, u32[]{:S(2)}) collective-permute-start(bf16[128,3072]{1,0:T(8,128)(2,1)S(1)} %all_gather.3.refs_0_), channel_id=1, source_target_pairs={{0,1},{1,0},{2,3},{3,2},{4,5},{5,4},{6,7},{7,6},{8,9},{9,8},{10,11... | collective-permute-start | bytes 2359304 | tf_op jit(solution)/shard_map/ppermute | solution.py:29
  60.5 18.7 %collective-permute-start.1 = (bf16[128,3072]{1,0:T(8,128)(2,1)S(1)}, bf16[128,3072]{1,0:T(8,128)(2,1)S(1)}, u32[]{:S(2)}, u32[]{:S(2)}) collective-permute-start(bf16[128,3072]{1,0:T(8,128)(2,1)S(1)} %all_gather.3.refs_0_), channel_id=1, source_target_pairs={{0,8},{1,25},{8,16},{9,1},{16,24},{17,9},{24,0},{25,17},{2,10},{3,... | collective-permute-start | bytes 2359304 | tf_op jit(solution)/shard_map/ppermute | solution.py:142
  64.9 19.6 %collective-permute-start.3 = (bf16[128,3072]{1,0:T(8,128)(2,1)S(1)}, bf16[128,3072]{1,0:T(8,128)(2,1)S(1)}, u32[]{:S(2)}, u32[]{:S(2)}) collective-permute-start(bf16[128,3072]{1,0:T(8,128)(2,1)S(1)} %all_gather.3.refs_0_), channel_id=1, source_target_pairs={{0,24},{1,9},{8,0},{9,17},{16,8},{17,25},{24,16},{25,1},{2,26},{3,... | collective-permute-start | bytes 2359304 | tf_op jit(solution)/shard_map/ppermute | solution.py:142
  66.9 1.2 %copy-start.1 = (bf16[1,512,1024]{2,1,0:T(8,128)(2,1)S(1)}, bf16[1,512,1024]{2,1,0:T(8,128)(2,1)}, u32[]{:S(2)}) copy-start(bf16[1,512,1024]{2,1,0:T(8,128)(2,1)} %param.9) | copy-start | bytes 3145732
  79.2 14.2 %collective-permute-start.2 = (bf16[128,3072]{1,0:T(8,128)(2,1)S(1)}, bf16[128,3072]{1,0:T(8,128)(2,1)S(1)}, u32[]{:S(2)}, u32[]{:S(2)}) collective-permute-start(bf16[128,3072]{1,0:T(8,128)(2,1)S(1)} %collective-permute-done.1.refs_0_), channel_id=1, source_target_pairs={{0,8},{1,25},{8,16},{9,1},{16,24},{17,9},{24,0},{25,17},{2,10},{3,... | collective-permute-start | bytes 2359304 | tf_op jit(solution)/shard_map/ppermute | solution.py:154
  84.5 12.7 %collective-permute-start.4 = (bf16[128,3072]{1,0:T(8,128)(2,1)S(1)}, bf16[128,3072]{1,0:T(8,128)(2,1)S(1)}, u32[]{:S(2)}, u32[]{:S(2)}) collective-permute-start(bf16[128,3072]{1,0:T(8,128)(2,1)S(1)} %collective-permute-done.3.refs_2_), channel_id=1, source_target_pairs={{0,1},{1,0},{2,3},{3,2},{4,5},{5,4},{6,7},{7,6},{8,9},{9,8},{10,11... | collective-permute-start | bytes 2359304 | tf_op jit(solution)/shard_map/ppermute | solution.py:29
  86.4 10.7 %collective-permute-start.5 = (bf16[128,3072]{1,0:T(8,128)(2,1)S(1)}, bf16[128,3072]{1,0:T(8,128)(2,1)S(1)}, u32[]{:S(2)}, u32[]{:S(2)}) collective-permute-start(bf16[128,3072]{1,0:T(8,128)(2,1)S(1)} %collective-permute-done.1.refs_0_), channel_id=1, source_target_pairs={{0,1},{1,0},{2,3},{3,2},{4,5},{5,4},{6,7},{7,6},{8,9},{9,8},{10,11... | collective-permute-start | bytes 2359304 | tf_op jit(solution)/shard_map/ppermute | solution.py:29
  93.4 5.6 %collective-permute-start.6 = (bf16[128,3072]{1,0:T(8,128)(2,1)S(1)}, bf16[128,3072]{1,0:T(8,128)(2,1)S(1)}, u32[]{:S(2)}, u32[]{:S(2)}) collective-permute-start(bf16[128,3072]{1,0:T(8,128)(2,1)S(1)} %collective-permute-done.2.mine_ref), channel_id=1, source_target_pairs={{0,1},{1,0},{2,3},{3,2},{4,5},{5,4},{6,7},{7,6},{8,9},{9,8},{10,11... | collective-permute-start | bytes 2359304 | tf_op jit(solution)/shard_map/ppermute | solution.py:29
  97.2 1.9 %copy-start.2 = (s32[1,4]{1,0:T(1,128)S(1)}, s32[1,4]{1,0:T(1,128)}, u32[]{:S(2)}) copy-start(s32[1,4]{1,0:T(1,128)} %param.10) | copy-start | bytes 52
  97.2 1.9 %copy-start.3 = (s32[1,4]{1,0:T(1,128)S(1)}, s32[1,4]{1,0:T(1,128)}, u32[]{:S(2)}) copy-start(s32[1,4]{1,0:T(1,128)} %param.11) | copy-start | bytes 52

commit v4 on v3

--- a/solution.py
+++ b/solution.py
@@ -139,7 +139,7 @@
     mine = lax.all_to_all(ordered, ("zl", "y"), split_axis=0, concat_axis=0, tiled=True)
     own = lax.all_gather(mine, "zh", axis=0, tiled=True)
     forth, back = x_ring(1), x_ring(-1)
-    first, second, own_other = forth(own), back(own), swap(own)
+    first, own_other = forth(own), swap(own)
     weights = weights[0]
     rows = weights.shape[0]
     where = jnp.stack([lax.axis_index("x"), lax.axis_index("c")]).astype(jnp.int32)
@@ -150,6 +150,8 @@
         [SMEM] + [VMEM] * 3,
         256,
     )(where, weights, own, own_other)
+    own, total = lax.optimization_barrier((own, total))
+    second = back(own)
     first, total = lax.optimization_barrier((first, total))
     far = forth(first)
     pieces = [first, swap(second), second, swap(first)]

time: 105 us -> 102 us (0.971)
  waiting for transfers between devices: 13.9 us -> 11.5 us
    ppermute x2, waiting for transfers between devices: 9.29 us -> 6.6 us  [the longest x1 6.24 us: per_device(): first, own_other = (forth(own), swap(own))]
  transfers between devices with their start and end apart: 7 -> 7, of which waited for: 2 -> 3; matrix products, arithmetic and copies ran while one was open for 0% -> 0% of each run, Pallas kernels for 3% -> 4%
where the time goes in v4:
time: 102 us
  blocking collectives  53 us (52%)
  starting transfers between devices  25.4 us (25%)
  waiting for transfers between devices  11.5 us (11%)
  Pallas kernels  9.18 us (9%)
  local copies, waits for them, and re-layouts  1.63 us (2%)
    all_gather x1, blocking collectives, per_device(): own = lax.all_gather(mine, 'zh', axis=0, tiled=True)  35.6 us
    all_to_all x1, blocking collectives, per_device(): lax.all_to_all(ordered, ('zl', 'y'), split_axis=0, concat_axis=0, tiled=T...  17.4 us
    ppermute x4, starting transfers between devices, swap(): return lax.ppermute(piece, 'c', [(0, 1), (1, 0)])  13.8 us
    ppermute x1, waiting for transfers between devices, per_device(): first, own_other = (forth(own), swap(own))  6.24 us
    pallas_call x1, Pallas kernels, per_device(): kernel_call(far_kernel, jax.ShapeDtypeStruct((rows, NT), jnp.bfloat16), [...  5.57 us
    ppermute x1, starting transfers between devices, per_device(): far = forth(first)  5.31 us
    ppermute x1, waiting for transfers between devices, per_device(): far = forth(first)  4.81 us
    ppermute x1, starting transfers between devices, per_device(): first, own_other = (forth(own), swap(own))  4.39 us
  transfers between devices with their start and end apart: 7, of which 3 were waited for; matrix products, arithmetic and copies ran while one was open for 0% of the time, Pallas kernels for 4%

profile of v4, /device:TPU:1, one launch (start us, length us, event | category | flops | bytes accessed | tf_op | source)
XLA Modules:
  0.0 101.8 jit_solution(188115912191816283)
XLA Ops:
  0.0 0.0 copy-start
  0.0 0.7 multiply_add_fusion
  0.7 0.2 copy-done
  1.0 0.2 convolution_convert_fusion
  1.1 0.1 all_to_all.8
  1.2 17.4 %all_to_all.12 = bf16[16,2,3072]{2,1,0:T(2,128)(2,1)S(1)} all-to-all(bf16[16,2,3072]{2,1,0:T(2,128)(2,1)S(1)} %all_to_all.8), channel_id=1, replica_groups=mesh['zl'=4,'y'=4,'x'=4,'zh'=4,'c'=2] {'zl','y'}, dimensions={0} | all-to-all | bytes 393216 | tf_op jit(solution)/shard_map/all_to_all | solution.py:139
  18.6 0.1 all_to_all.10
  18.7 35.6 %all_gather.3.refs_0_ = bf16[128,3072]{1,0:T(8,128)(2,1)S(1)} all-gather(bf16[32,3072]{1,0:T(8,128)(2,1)S(1)} %all_to_all.10), channel_id=1, replica_groups=mesh['zl'=4,'y'=4,'x'=4,'zh'=4,'c'=2] {'zh'}, dimensions={0}, use_global_device_ids=true | all-gather | bytes 983040 | tf_op jit(solution)/shard_map/all_gather | solution.py:140
  54.3 6.1 %collective-permute-start = (bf16[128,3072]{1,0:T(8,128)(2,1)S(1)}, bf16[128,3072]{1,0:T(8,128)(2,1)S(1)}, u32[]{:S(2)}, u32[]{:S(2)}) collective-permute-start(bf16[128,3072]{1,0:T(8,128)(2,1)S(1)} %all_gather.3.refs_0_), channel_id=1, source_target_pairs={{0,1},{1,0},{2,3},{3,2},{4,5},{5,4},{6,7},{7,6},{8,9},{9,8},{10,11... | collective-permute-start | bytes 2359304 | tf_op jit(solution)/shard_map/ppermute | solution.py:29
  60.5 4.4 %collective-permute-start.1 = (bf16[128,3072]{1,0:T(8,128)(2,1)S(1)}, bf16[128,3072]{1,0:T(8,128)(2,1)S(1)}, u32[]{:S(2)}, u32[]{:S(2)}) collective-permute-start(bf16[128,3072]{1,0:T(8,128)(2,1)S(1)} %all_gather.3.refs_0_), channel_id=1, source_target_pairs={{0,8},{1,25},{8,16},{9,1},{16,24},{17,9},{24,0},{25,17},{2,10},{3,... | collective-permute-start | bytes 2359304 | tf_op jit(solution)/shard_map/ppermute | solution.py:142
  64.9 0.1 pad_add_fusion.where_ref
  64.9 0.0 collective-permute-done.refs_1_
  64.9 0.0 copy-start.1
  64.9 1.2 %copy-done.1 = bf16[1,512,1024]{2,1,0:T(8,128)(2,1)S(1)} copy-done((bf16[1,512,1024]{2,1,0:T(8,128)(2,1)S(1)}, bf16[1,512,1024]{2,1,0:T(8,128)(2,1)}, u32[]{:S(2)}) %copy-start.1) | copy-done | bytes 1048600
  66.2 1.8 %shard_map.64 = (f32[512,3072]{1,0:T(8,128)S(1)}, bf16[512,1024]{1,0:T(8,128)(2,1)S(1)}) custom-call(s32[2]{0:T(128)S(1)} %pad_add_fusion.where_ref, bf16[512,1024]{1,0:T(8,128)(2,1)S(1)} %bitcast.7, bf16[128,3072]{1,0:T(8,128)(2,1)S(1)} %all_gather.3.refs_0_, bf16[128,3072]{1,0:T(8,128)(2,1)S(1)} %collective-permute-done.refs_1_), custom_call_target="tpu_custom_call" | custom-call | flops 3145728 | bytes 256 | tf_op jit(solution)/shard_map/pallas_call | solution.py:147
  68.0 1.9 %collective-permute-start.3 = (bf16[128,3072]{1,0:T(8,128)(2,1)S(1)}, bf16[128,3072]{1,0:T(8,128)(2,1)S(1)}, u32[]{:S(2)}, u32[]{:S(2)}) collective-permute-start(bf16[128,3072]{1,0:T(8,128)(2,1)S(1)} %all_gather.3.refs_0_), channel_id=1, source_target_pairs={{0,24},{1,9},{8,0},{9,17},{16,8},{17,25},{24,16},{25,1},{2,26},{3,... | collective-permute-start | bytes 2359304 | tf_op jit(solution)/shard_map/ppermute | solution.py:154
  69.9 6.2 %collective-permute-done.1.refs_0_ = bf16[128,3072]{1,0:T(8,128)(2,1)S(1)} collective-permute-done((bf16[128,3072]{1,0:T(8,128)(2,1)S(1)}, bf16[128,3072]{1,0:T(8,128)(2,1)S(1)}, u32[]{:S(2)}, u32[]{:S(2)}) %collective-permute-start.1) | collective-permute-done | bytes 786464 | tf_op jit(solution)/shard_map/ppermute | solution.py:142
  76.1 5.3 %collective-permute-start.2 = (bf16[128,3072]{1,0:T(8,128)(2,1)S(1)}, bf16[128,3072]{1,0:T(8,128)(2,1)S(1)}, u32[]{:S(2)}, u32[]{:S(2)}) collective-permute-start(bf16[128,3072]{1,0:T(8,128)(2,1)S(1)} %collective-permute-done.1.refs_0_), channel_id=1, source_target_pairs={{0,8},{1,25},{8,16},{9,1},{16,24},{17,9},{24,0},{25,17},{2,10},{3,... | collective-permute-start | bytes 2359304 | tf_op jit(solution)/shard_map/ppermute | solution.py:156
  81.5 1.9 %collective-permute-start.5 = (bf16[128,3072]{1,0:T(8,128)(2,1)S(1)}, bf16[128,3072]{1,0:T(8,128)(2,1)S(1)}, u32[]{:S(2)}, u32[]{:S(2)}) collective-permute-start(bf16[128,3072]{1,0:T(8,128)(2,1)S(1)} %collective-permute-done.1.refs_0_), channel_id=1, source_target_pairs={{0,1},{1,0},{2,3},{3,2},{4,5},{5,4},{6,7},{7,6},{8,9},{9,8},{10,11... | collective-permute-start | bytes 2359304 | tf_op jit(solution)/shard_map/ppermute | solution.py:29
  83.4 0.4 collective-permute-done.3.refs_2_
  83.7 2.1 %collective-permute-start.4 = (bf16[128,3072]{1,0:T(8,128)(2,1)S(1)}, bf16[128,3072]{1,0:T(8,128)(2,1)S(1)}, u32[]{:S(2)}, u32[]{:S(2)}) collective-permute-start(bf16[128,3072]{1,0:T(8,128)(2,1)S(1)} %collective-permute-done.3.refs_2_), channel_id=1, source_target_pairs={{0,1},{1,0},{2,3},{3,2},{4,5},{5,4},{6,7},{7,6},{8,9},{9,8},{10,11... | collective-permute-start | bytes 2359304 | tf_op jit(solution)/shard_map/ppermute | solution.py:29
  85.8 4.8 %collective-permute-done.2.mine_ref = bf16[128,3072]{1,0:T(8,128)(2,1)S(1)} collective-permute-done((bf16[128,3072]{1,0:T(8,128)(2,1)S(1)}, bf16[128,3072]{1,0:T(8,128)(2,1)S(1)}, u32[]{:S(2)}, u32[]{:S(2)}) %collective-permute-start.2) | collective-permute-done | bytes 786464 | tf_op jit(solution)/shard_map/ppermute | solution.py:156
  90.6 3.7 %collective-permute-start.6 = (bf16[128,3072]{1,0:T(8,128)(2,1)S(1)}, bf16[128,3072]{1,0:T(8,128)(2,1)S(1)}, u32[]{:S(2)}, u32[]{:S(2)}) collective-permute-start(bf16[128,3072]{1,0:T(8,128)(2,1)S(1)} %collective-permute-done.2.mine_ref), channel_id=1, source_target_pairs={{0,1},{1,0},{2,3},{3,2},{4,5},{5,4},{6,7},{7,6},{8,9},{9,8},{10,11... | collective-permute-start | bytes 2359304 | tf_op jit(solution)/shard_map/ppermute | solution.py:29
  94.3 0.0 collective-permute-done.5.refs_3_
  94.3 0.0 collective-permute-done.4.refs_1_
  94.3 0.0 copy-start.2
  94.4 0.0 copy-start.3
  94.4 1.8 %shard_map.65.near_ref = f32[512,3072]{1,0:T(8,128)S(1)} custom-call(bf16[512,1024]{1,0:T(8,128)(2,1)S(1)} %get-tuple-element.13.weights_ref, f32[512,3072]{1,0:T(8,128)S(1)} %get-tuple-element.18.product_ref, bf16[128,3072]{1,0:T(8,128)(2,1)S(1)} %collective-permute-done.1.refs_0_, bf16[128,3072]{1,0:T(8,128)(2,1)S(1)} %collective-permute-done.4.refs_1_, ...), custom_call_target="tpu_custom_call" | custom-call | flops 6291456 | bytes 512 | tf_op jit(solution)/shard_map/pallas_call | solution.py:159
  96.2 0.0 collective-permute-done.6.theirs_ref
  96.2 0.0 copy-done.2
  96.2 0.0 copy-done.3
  96.2 5.6 %shard_map.66 = bf16[512,1536]{1,0:T(8,128)(2,1)} custom-call(s32[4]{0:T(128)S(1)} %bitcast.8, s32[4]{0:T(128)S(1)} %bitcast.9, bf16[512,1024]{1,0:T(8,128)(2,1)S(1)} %get-tuple-element.13.weights_ref, f32[512,3072]{1,0:T(8,128)S(1)} %shard_map.65.near_ref, bf16[128,3072]{1,0:T(8,128)(2,1)S(1)} %collective-permute-done.2.mine_ref, ...), custom_call_target="tpu_custom_call" | custom-call | flops 3145728 | bytes 256 | tf_op jit(solution)/shard_map/pallas_call | solution.py:160
Async XLA Ops:
  0.0 1.0 copy-start
  54.3 10.6 %collective-permute-start = (bf16[128,3072]{1,0:T(8,128)(2,1)S(1)}, bf16[128,3072]{1,0:T(8,128)(2,1)S(1)}, u32[]{:S(2)}, u32[]{:S(2)}) collective-permute-start(bf16[128,3072]{1,0:T(8,128)(2,1)S(1)} %all_gather.3.refs_0_), channel_id=1, source_target_pairs={{0,1},{1,0},{2,3},{3,2},{4,5},{5,4},{6,7},{7,6},{8,9},{9,8},{10,11... | collective-permute-start | bytes 2359304 | tf_op jit(solution)/shard_map/ppermute | solution.py:29
  60.5 15.7 %collective-permute-start.1 = (bf16[128,3072]{1,0:T(8,128)(2,1)S(1)}, bf16[128,3072]{1,0:T(8,128)(2,1)S(1)}, u32[]{:S(2)}, u32[]{:S(2)}) collective-permute-start(bf16[128,3072]{1,0:T(8,128)(2,1)S(1)} %all_gather.3.refs_0_), channel_id=1, source_target_pairs={{0,8},{1,25},{8,16},{9,1},{16,24},{17,9},{24,0},{25,17},{2,10},{3,... | collective-permute-start | bytes 2359304 | tf_op jit(solution)/shard_map/ppermute | solution.py:142
  64.9 1.2 %copy-start.1 = (bf16[1,512,1024]{2,1,0:T(8,128)(2,1)S(1)}, bf16[1,512,1024]{2,1,0:T(8,128)(2,1)}, u32[]{:S(2)}) copy-start(bf16[1,512,1024]{2,1,0:T(8,128)(2,1)} %param.9) | copy-start | bytes 3145732
  68.0 15.8 %collective-permute-start.3 = (bf16[128,3072]{1,0:T(8,128)(2,1)S(1)}, bf16[128,3072]{1,0:T(8,128)(2,1)S(1)}, u32[]{:S(2)}, u32[]{:S(2)}) collective-permute-start(bf16[128,3072]{1,0:T(8,128)(2,1)S(1)} %all_gather.3.refs_0_), channel_id=1, source_target_pairs={{0,24},{1,9},{8,0},{9,17},{16,8},{17,25},{24,16},{25,1},{2,26},{3,... | collective-permute-start | bytes 2359304 | tf_op jit(solution)/shard_map/ppermute | solution.py:154
  76.1 14.5 %collective-permute-start.2 = (bf16[128,3072]{1,0:T(8,128)(2,1)S(1)}, bf16[128,3072]{1,0:T(8,128)(2,1)S(1)}, u32[]{:S(2)}, u32[]{:S(2)}) collective-permute-start(bf16[128,3072]{1,0:T(8,128)(2,1)S(1)} %collective-permute-done.1.refs_0_), channel_id=1, source_target_pairs={{0,8},{1,25},{8,16},{9,1},{16,24},{17,9},{24,0},{25,17},{2,10},{3,... | collective-permute-start | bytes 2359304 | tf_op jit(solution)/shard_map/ppermute | solution.py:156
  81.5 12.9 %collective-permute-start.5 = (bf16[128,3072]{1,0:T(8,128)(2,1)S(1)}, bf16[128,3072]{1,0:T(8,128)(2,1)S(1)}, u32[]{:S(2)}, u32[]{:S(2)}) collective-permute-start(bf16[128,3072]{1,0:T(8,128)(2,1)S(1)} %collective-permute-done.1.refs_0_), channel_id=1, source_target_pairs={{0,1},{1,0},{2,3},{3,2},{4,5},{5,4},{6,7},{7,6},{8,9},{9,8},{10,11... | collective-permute-start | bytes 2359304 | tf_op jit(solution)/shard_map/ppermute | solution.py:29
  83.7 10.6 %collective-permute-start.4 = (bf16[128,3072]{1,0:T(8,128)(2,1)S(1)}, bf16[128,3072]{1,0:T(8,128)(2,1)S(1)}, u32[]{:S(2)}, u32[]{:S(2)}) collective-permute-start(bf16[128,3072]{1,0:T(8,128)(2,1)S(1)} %collective-permute-done.3.refs_2_), channel_id=1, source_target_pairs={{0,1},{1,0},{2,3},{3,2},{4,5},{5,4},{6,7},{7,6},{8,9},{9,8},{10,11... | collective-permute-start | bytes 2359304 | tf_op jit(solution)/shard_map/ppermute | solution.py:29
  90.6 5.6 %collective-permute-start.6 = (bf16[128,3072]{1,0:T(8,128)(2,1)S(1)}, bf16[128,3072]{1,0:T(8,128)(2,1)S(1)}, u32[]{:S(2)}, u32[]{:S(2)}) collective-permute-start(bf16[128,3072]{1,0:T(8,128)(2,1)S(1)} %collective-permute-done.2.mine_ref), channel_id=1, source_target_pairs={{0,1},{1,0},{2,3},{3,2},{4,5},{5,4},{6,7},{7,6},{8,9},{9,8},{10,11... | collective-permute-start | bytes 2359304 | tf_op jit(solution)/shard_map/ppermute | solution.py:29
  94.3 1.9 %copy-start.2 = (s32[1,4]{1,0:T(1,128)S(1)}, s32[1,4]{1,0:T(1,128)}, u32[]{:S(2)}) copy-start(s32[1,4]{1,0:T(1,128)} %param.10) | copy-start | bytes 52
  94.4 1.9 %copy-start.3 = (s32[1,4]{1,0:T(1,128)S(1)}, s32[1,4]{1,0:T(1,128)}, u32[]{:S(2)}) copy-start(s32[1,4]{1,0:T(1,128)} %param.11) | copy-start | bytes 52

commit v5 on v4

--- a/solution.py
+++ b/solution.py
@@ -63,8 +63,56 @@
     )
 
 
-def far_kernel(band_ref, level_ref, weights_ref, near_ref, mine_ref, theirs_ref, out_ref, *products):
+def turned_taps(product, rows, start, reach, scale, out_ref):
     lane = lax.broadcasted_iota(jnp.int32, (CB, LANES), 1)
+    turned, keeps = [], []
+    for at in (start, start - reach, start + reach):
+        tile = at // LANES
+        fine = at - tile * LANES
+        wide = product[:, pl.ds(pl.multiple_of(tile * LANES, LANES), NT + LANES)]
+        back = lax.rem(LANES - fine, LANES)
+        turned.append(
+            [
+                pltpu.roll(wide[:, k * LANES : (k + 1) * LANES], back, 1)
+                for k in range(NT // LANES + 1)
+            ]
+        )
+        keeps.append(lane < LANES - fine)
+    for k in range(NT // LANES):
+        middle, left, right = [
+            jnp.where(keep, tiles[k], tiles[k + 1]) for keep, tiles in zip(keeps, turned)
+        ]
+        out_ref[rows, k * LANES : (k + 1) * LANES] = (
+            (middle - 0.5 * (left + right)) * scale
+        ).astype(out_ref.dtype)
+
+
+def banded_taps(product, rows, start, reach, scale, out_ref):
+    tile = (start - 3) // LANES
+    fine = start - tile * LANES
+    wide = product[:, pl.ds(pl.multiple_of(tile * LANES, LANES), SPAN)]
+    high = wide.astype(jnp.bfloat16)
+    low = (wide - high.astype(jnp.float32)).astype(jnp.bfloat16)
+    offset = (
+        lax.broadcasted_iota(jnp.int32, (4 * LANES, 2 * LANES), 0)
+        - lax.broadcasted_iota(jnp.int32, (4 * LANES, 2 * LANES), 1)
+        - fine
+    )
+    taps = jnp.where(
+        offset == 0, 1.0, jnp.where((offset == reach) | (offset == -reach), -0.5, 0.0)
+    ).astype(jnp.bfloat16)
+    for at in range(0, NT, 2 * LANES):
+        part = slice(at, at + 4 * LANES)
+        result = jnp.dot(high[:, part], taps, preferred_element_type=jnp.float32) + jnp.dot(
+            low[:, part], taps, preferred_element_type=jnp.float32
+        )
+        out_ref[rows, at : at + 2 * LANES] = (result * scale).astype(out_ref.dtype)
+
+
+def far_kernel(band_ref, level_ref, weights_ref, near_ref, mine_ref, theirs_ref, out_hbm, *refs):
+    *products, out_ref, sems = refs
+    lane = lax.broadcasted_iota(jnp.int32, (CB, LANES), 1)
+    copies = []
     for block, product in enumerate(products):
         rows = slice(block * CB, (block + 1) * CB)
         at = jnp.clip((band_ref[block] - 3 + LANES) // LANES - 1, 0, (NS - SPAN) // LANES)
@@ -84,43 +132,33 @@
             lane == 1, -last, jnp.where(lane == 2, -2.0 * last, 0.0)
         )
         product[:, 2 * LANES + NS :] = jnp.zeros((CB, 2 * LANES), jnp.float32)
-
-        start = band_ref[block] + LANES
         smooth = level_ref[block] > 0
-        reach = jnp.where(smooth, 3, 1)
-        scale = jnp.where(smooth, 1.0 / 9.0, 1.0)
-        turned, keeps = [], []
-        for at in (start, start - reach, start + reach):
-            tile = at // LANES
-            fine = at - tile * LANES
-            wide = product[:, pl.ds(pl.multiple_of(tile * LANES, LANES), NT + LANES)]
-            back = lax.rem(LANES - fine, LANES)
-            turned.append(
-                [
-                    pltpu.roll(wide[:, k * LANES : (k + 1) * LANES], back, 1)
-                    for k in range(NT // LANES + 1)
-                ]
-            )
-            keeps.append(lane < LANES - fine)
-        for k in range(NT // LANES):
-            middle, left, right = [
-                jnp.where(keep, tiles[k], tiles[k + 1]) for keep, tiles in zip(keeps, turned)
-            ]
-            out_ref[rows, k * LANES : (k + 1) * LANES] = (
-                (middle - 0.5 * (left + right)) * scale
-            ).astype(out_ref.dtype)
+        taps = turned_taps if block % 2 == 0 else banded_taps
+        taps(
+            product,
+            rows,
+            band_ref[block] + LANES,
+            jnp.where(smooth, 3, 1),
+            jnp.where(smooth, 1.0 / 9.0, 1.0),
+            out_ref,
+        )
+        copy = pltpu.make_async_copy(out_ref.at[rows], out_hbm.at[rows], sems.at[block])
+        copy.start()
+        copies.append(copy)
+    for copy in copies:
+        copy.wait()
 
 
 SMEM = pl.BlockSpec(memory_space=pltpu.SMEM)
 VMEM = pl.BlockSpec(memory_space=pltpu.VMEM)
 
 
-def kernel_call(body, outs, in_specs, depth, scratch=()):
+def kernel_call(body, outs, in_specs, depth, scratch=(), place=VMEM):
     return pl.pallas_call(
         body,
         out_shape=outs,
         in_specs=in_specs,
-        out_specs=jax.tree.map(lambda _: VMEM, outs),
+        out_specs=jax.tree.map(lambda _: place, outs),
         scratch_shapes=list(scratch),
         compiler_params=pltpu.CompilerParams(vmem_limit_bytes=16 << 20),
         cost_estimate=pl.CostEstimate(
@@ -162,7 +200,9 @@
         jax.ShapeDtypeStruct((rows, NT), jnp.bfloat16),
         [SMEM] * 2 + [VMEM] * 4,
         256,
-        [pltpu.VMEM((CB, PADDED), jnp.float32)] * (rows // CB),
+        [pltpu.VMEM((CB, PADDED), jnp.float32)] * (rows // CB)
+        + [pltpu.VMEM((rows, NT), jnp.bfloat16), pltpu.SemaphoreType.DMA((rows // CB,))],
+        pl.BlockSpec(memory_space=pl.ANY),
     )(band_start[0], smoothing[0], weights, total, far, swap(far))[None]
 
 

time: 102 us -> 101 us (level)
  no operation moved by 1% of the time
where the time goes in v5:
time: 101 us
  blocking collectives  53 us (52%)
  starting transfers between devices  25.4 us (25%)
  waiting for transfers between devices  11.4 us (11%)
  Pallas kernels  8.19 us (8%)
  local copies, waits for them, and re-layouts  1.63 us (2%)
    all_gather x1, blocking collectives, per_device(): own = lax.all_gather(mine, 'zh', axis=0, tiled=True)  35.6 us
    all_to_all x1, blocking collectives, per_device(): lax.all_to_all(ordered, ('zl', 'y'), split_axis=0, concat_axis=0, tiled=T...  17.4 us
    ppermute x4, starting transfers between devices, swap(): return lax.ppermute(piece, 'c', [(0, 1), (1, 0)])  13.8 us
    ppermute x1, waiting for transfers between devices, per_device(): first, own_other = (forth(own), swap(own))  6.24 us
    ppermute x1, starting transfers between devices, per_device(): far = forth(first)  5.31 us
    ppermute x1, waiting for transfers between devices, per_device(): far = forth(first)  4.81 us
    pallas_call x1, Pallas kernels, per_device(): kernel_call(far_kernel, jax.ShapeDtypeStruct((rows, NT), jnp.bfloat16), [...  4.58 us
    ppermute x1, starting transfers between devices, per_device(): first, own_other = (forth(own), swap(own))  4.39 us
  transfers between devices with their start and end apart: 7, of which 3 were waited for; matrix products, arithmetic and copies ran while one was open for 0% of the time, Pallas kernels for 4%

profile of v5, /device:TPU:1, one launch (start us, length us, event | category | flops | bytes accessed | tf_op | source)
XLA Modules:
  0.0 100.8 jit_solution(12385794298560712475)
XLA Ops:
  0.0 0.0 copy-start
  0.0 0.7 multiply_add_fusion
  0.7 0.2 copy-done
  1.0 0.2 convolution_convert_fusion
  1.1 0.1 all_to_all.8
  1.2 17.4 %all_to_all.12 = bf16[16,2,3072]{2,1,0:T(2,128)(2,1)S(1)} all-to-all(bf16[16,2,3072]{2,1,0:T(2,128)(2,1)S(1)} %all_to_all.8), channel_id=1, replica_groups=mesh['zl'=4,'y'=4,'x'=4,'zh'=4,'c'=2] {'zl','y'}, dimensions={0} | all-to-all | bytes 393216 | tf_op jit(solution)/shard_map/all_to_all | solution.py:177
  18.6 0.1 all_to_all.10
  18.7 35.6 %all_gather.3.refs_0_ = bf16[128,3072]{1,0:T(8,128)(2,1)S(1)} all-gather(bf16[32,3072]{1,0:T(8,128)(2,1)S(1)} %all_to_all.10), channel_id=1, replica_groups=mesh['zl'=4,'y'=4,'x'=4,'zh'=4,'c'=2] {'zh'}, dimensions={0}, use_global_device_ids=true | all-gather | bytes 983040 | tf_op jit(solution)/shard_map/all_gather | solution.py:178
  54.3 6.1 %collective-permute-start = (bf16[128,3072]{1,0:T(8,128)(2,1)S(1)}, bf16[128,3072]{1,0:T(8,128)(2,1)S(1)}, u32[]{:S(2)}, u32[]{:S(2)}) collective-permute-start(bf16[128,3072]{1,0:T(8,128)(2,1)S(1)} %all_gather.3.refs_0_), channel_id=1, source_target_pairs={{0,1},{1,0},{2,3},{3,2},{4,5},{5,4},{6,7},{7,6},{8,9},{9,8},{10,11... | collective-permute-start | bytes 2359304 | tf_op jit(solution)/shard_map/ppermute | solution.py:29
  60.5 4.4 %collective-permute-start.1 = (bf16[128,3072]{1,0:T(8,128)(2,1)S(1)}, bf16[128,3072]{1,0:T(8,128)(2,1)S(1)}, u32[]{:S(2)}, u32[]{:S(2)}) collective-permute-start(bf16[128,3072]{1,0:T(8,128)(2,1)S(1)} %all_gather.3.refs_0_), channel_id=1, source_target_pairs={{0,8},{1,25},{8,16},{9,1},{16,24},{17,9},{24,0},{25,17},{2,10},{3,... | collective-permute-start | bytes 2359304 | tf_op jit(solution)/shard_map/ppermute | solution.py:180
  64.9 0.1 pad_add_fusion.where_ref
  64.9 0.0 collective-permute-done.refs_1_
  64.9 0.0 copy-start.1
  64.9 1.2 %copy-done.1 = bf16[1,512,1024]{2,1,0:T(8,128)(2,1)S(1)} copy-done((bf16[1,512,1024]{2,1,0:T(8,128)(2,1)S(1)}, bf16[1,512,1024]{2,1,0:T(8,128)(2,1)}, u32[]{:S(2)}) %copy-start.1) | copy-done | bytes 1048600
  66.2 1.8 %shard_map.64 = (f32[512,3072]{1,0:T(8,128)S(1)}, bf16[512,1024]{1,0:T(8,128)(2,1)S(1)}) custom-call(s32[2]{0:T(128)S(1)} %pad_add_fusion.where_ref, bf16[512,1024]{1,0:T(8,128)(2,1)S(1)} %bitcast.7, bf16[128,3072]{1,0:T(8,128)(2,1)S(1)} %all_gather.3.refs_0_, bf16[128,3072]{1,0:T(8,128)(2,1)S(1)} %collective-permute-done.refs_1_), custom_call_target="tpu_custom_call" | custom-call | flops 3145728 | bytes 256 | tf_op jit(solution)/shard_map/pallas_call | solution.py:185
  68.0 1.9 %collective-permute-start.3 = (bf16[128,3072]{1,0:T(8,128)(2,1)S(1)}, bf16[128,3072]{1,0:T(8,128)(2,1)S(1)}, u32[]{:S(2)}, u32[]{:S(2)}) collective-permute-start(bf16[128,3072]{1,0:T(8,128)(2,1)S(1)} %all_gather.3.refs_0_), channel_id=1, source_target_pairs={{0,24},{1,9},{8,0},{9,17},{16,8},{17,25},{24,16},{25,1},{2,26},{3,... | collective-permute-start | bytes 2359304 | tf_op jit(solution)/shard_map/ppermute | solution.py:192
  69.9 6.2 %collective-permute-done.1.refs_0_ = bf16[128,3072]{1,0:T(8,128)(2,1)S(1)} collective-permute-done((bf16[128,3072]{1,0:T(8,128)(2,1)S(1)}, bf16[128,3072]{1,0:T(8,128)(2,1)S(1)}, u32[]{:S(2)}, u32[]{:S(2)}) %collective-permute-start.1) | collective-permute-done | bytes 786464 | tf_op jit(solution)/shard_map/ppermute | solution.py:180
  76.1 5.3 %collective-permute-start.2 = (bf16[128,3072]{1,0:T(8,128)(2,1)S(1)}, bf16[128,3072]{1,0:T(8,128)(2,1)S(1)}, u32[]{:S(2)}, u32[]{:S(2)}) collective-permute-start(bf16[128,3072]{1,0:T(8,128)(2,1)S(1)} %collective-permute-done.1.refs_0_), channel_id=1, source_target_pairs={{0,8},{1,25},{8,16},{9,1},{16,24},{17,9},{24,0},{25,17},{2,10},{3,... | collective-permute-start | bytes 2359304 | tf_op jit(solution)/shard_map/ppermute | solution.py:194
  81.5 1.9 %collective-permute-start.5 = (bf16[128,3072]{1,0:T(8,128)(2,1)S(1)}, bf16[128,3072]{1,0:T(8,128)(2,1)S(1)}, u32[]{:S(2)}, u32[]{:S(2)}) collective-permute-start(bf16[128,3072]{1,0:T(8,128)(2,1)S(1)} %collective-permute-done.1.refs_0_), channel_id=1, source_target_pairs={{0,1},{1,0},{2,3},{3,2},{4,5},{5,4},{6,7},{7,6},{8,9},{9,8},{10,11... | collective-permute-start | bytes 2359304 | tf_op jit(solution)/shard_map/ppermute | solution.py:29
  83.4 0.4 collective-permute-done.3.refs_2_
  83.7 2.1 %collective-permute-start.4 = (bf16[128,3072]{1,0:T(8,128)(2,1)S(1)}, bf16[128,3072]{1,0:T(8,128)(2,1)S(1)}, u32[]{:S(2)}, u32[]{:S(2)}) collective-permute-start(bf16[128,3072]{1,0:T(8,128)(2,1)S(1)} %collective-permute-done.3.refs_2_), channel_id=1, source_target_pairs={{0,1},{1,0},{2,3},{3,2},{4,5},{5,4},{6,7},{7,6},{8,9},{9,8},{10,11... | collective-permute-start | bytes 2359304 | tf_op jit(solution)/shard_map/ppermute | solution.py:29
  85.8 4.8 %collective-permute-done.2.mine_ref = bf16[128,3072]{1,0:T(8,128)(2,1)S(1)} collective-permute-done((bf16[128,3072]{1,0:T(8,128)(2,1)S(1)}, bf16[128,3072]{1,0:T(8,128)(2,1)S(1)}, u32[]{:S(2)}, u32[]{:S(2)}) %collective-permute-start.2) | collective-permute-done | bytes 786464 | tf_op jit(solution)/shard_map/ppermute | solution.py:194
  90.6 3.7 %collective-permute-start.6 = (bf16[128,3072]{1,0:T(8,128)(2,1)S(1)}, bf16[128,3072]{1,0:T(8,128)(2,1)S(1)}, u32[]{:S(2)}, u32[]{:S(2)}) collective-permute-start(bf16[128,3072]{1,0:T(8,128)(2,1)S(1)} %collective-permute-done.2.mine_ref), channel_id=1, source_target_pairs={{0,1},{1,0},{2,3},{3,2},{4,5},{5,4},{6,7},{7,6},{8,9},{9,8},{10,11... | collective-permute-start | bytes 2359304 | tf_op jit(solution)/shard_map/ppermute | solution.py:29
  94.3 0.0 collective-permute-done.5.refs_3_
  94.3 0.0 collective-permute-done.4.refs_1_
  94.3 0.0 copy-start.2
  94.4 0.0 copy-start.3
  94.4 1.8 %shard_map.65.near_ref = f32[512,3072]{1,0:T(8,128)S(1)} custom-call(bf16[512,1024]{1,0:T(8,128)(2,1)S(1)} %get-tuple-element.13.weights_ref, f32[512,3072]{1,0:T(8,128)S(1)} %get-tuple-element.18.product_ref, bf16[128,3072]{1,0:T(8,128)(2,1)S(1)} %collective-permute-done.1.refs_0_, bf16[128,3072]{1,0:T(8,128)(2,1)S(1)} %collective-permute-done.4.refs_1_, ...), custom_call_target="tpu_custom_call" | custom-call | flops 6291456 | bytes 512 | tf_op jit(solution)/shard_map/pallas_call | solution.py:197
  96.2 0.0 collective-permute-done.6.theirs_ref
  96.2 0.0 copy-done.2
  96.2 0.0 copy-done.3
  96.2 4.6 %shard_map.66 = bf16[512,1536]{1,0:T(8,128)(2,1)} custom-call(s32[4]{0:T(128)S(1)} %bitcast.8, s32[4]{0:T(128)S(1)} %bitcast.9, bf16[512,1024]{1,0:T(8,128)(2,1)S(1)} %get-tuple-element.13.weights_ref, f32[512,3072]{1,0:T(8,128)S(1)} %shard_map.65.near_ref, bf16[128,3072]{1,0:T(8,128)(2,1)S(1)} %collective-permute-done.2.mine_ref, ...), custom_call_target="tpu_custom_call" | custom-call | flops 3145728 | bytes 256 | tf_op jit(solution)/shard_map/pallas_call | solution.py:198
Async XLA Ops:
  0.0 1.0 copy-start
  54.3 10.6 %collective-permute-start = (bf16[128,3072]{1,0:T(8,128)(2,1)S(1)}, bf16[128,3072]{1,0:T(8,128)(2,1)S(1)}, u32[]{:S(2)}, u32[]{:S(2)}) collective-permute-start(bf16[128,3072]{1,0:T(8,128)(2,1)S(1)} %all_gather.3.refs_0_), channel_id=1, source_target_pairs={{0,1},{1,0},{2,3},{3,2},{4,5},{5,4},{6,7},{7,6},{8,9},{9,8},{10,11... | collective-permute-start | bytes 2359304 | tf_op jit(solution)/shard_map/ppermute | solution.py:29
  60.5 15.7 %collective-permute-start.1 = (bf16[128,3072]{1,0:T(8,128)(2,1)S(1)}, bf16[128,3072]{1,0:T(8,128)(2,1)S(1)}, u32[]{:S(2)}, u32[]{:S(2)}) collective-permute-start(bf16[128,3072]{1,0:T(8,128)(2,1)S(1)} %all_gather.3.refs_0_), channel_id=1, source_target_pairs={{0,8},{1,25},{8,16},{9,1},{16,24},{17,9},{24,0},{25,17},{2,10},{3,... | collective-permute-start | bytes 2359304 | tf_op jit(solution)/shard_map/ppermute | solution.py:180
  64.9 1.2 %copy-start.1 = (bf16[1,512,1024]{2,1,0:T(8,128)(2,1)S(1)}, bf16[1,512,1024]{2,1,0:T(8,128)(2,1)}, u32[]{:S(2)}) copy-start(bf16[1,512,1024]{2,1,0:T(8,128)(2,1)} %param.9) | copy-start | bytes 3145732
  68.0 15.8 %collective-permute-start.3 = (bf16[128,3072]{1,0:T(8,128)(2,1)S(1)}, bf16[128,3072]{1,0:T(8,128)(2,1)S(1)}, u32[]{:S(2)}, u32[]{:S(2)}) collective-permute-start(bf16[128,3072]{1,0:T(8,128)(2,1)S(1)} %all_gather.3.refs_0_), channel_id=1, source_target_pairs={{0,24},{1,9},{8,0},{9,17},{16,8},{17,25},{24,16},{25,1},{2,26},{3,... | collective-permute-start | bytes 2359304 | tf_op jit(solution)/shard_map/ppermute | solution.py:192
  76.1 14.5 %collective-permute-start.2 = (bf16[128,3072]{1,0:T(8,128)(2,1)S(1)}, bf16[128,3072]{1,0:T(8,128)(2,1)S(1)}, u32[]{:S(2)}, u32[]{:S(2)}) collective-permute-start(bf16[128,3072]{1,0:T(8,128)(2,1)S(1)} %collective-permute-done.1.refs_0_), channel_id=1, source_target_pairs={{0,8},{1,25},{8,16},{9,1},{16,24},{17,9},{24,0},{25,17},{2,10},{3,... | collective-permute-start | bytes 2359304 | tf_op jit(solution)/shard_map/ppermute | solution.py:194
  81.5 12.9 %collective-permute-start.5 = (bf16[128,3072]{1,0:T(8,128)(2,1)S(1)}, bf16[128,3072]{1,0:T(8,128)(2,1)S(1)}, u32[]{:S(2)}, u32[]{:S(2)}) collective-permute-start(bf16[128,3072]{1,0:T(8,128)(2,1)S(1)} %collective-permute-done.1.refs_0_), channel_id=1, source_target_pairs={{0,1},{1,0},{2,3},{3,2},{4,5},{5,4},{6,7},{7,6},{8,9},{9,8},{10,11... | collective-permute-start | bytes 2359304 | tf_op jit(solution)/shard_map/ppermute | solution.py:29
  83.7 10.6 %collective-permute-start.4 = (bf16[128,3072]{1,0:T(8,128)(2,1)S(1)}, bf16[128,3072]{1,0:T(8,128)(2,1)S(1)}, u32[]{:S(2)}, u32[]{:S(2)}) collective-permute-start(bf16[128,3072]{1,0:T(8,128)(2,1)S(1)} %collective-permute-done.3.refs_2_), channel_id=1, source_target_pairs={{0,1},{1,0},{2,3},{3,2},{4,5},{5,4},{6,7},{7,6},{8,9},{9,8},{10,11... | collective-permute-start | bytes 2359304 | tf_op jit(solution)/shard_map/ppermute | solution.py:29
  90.6 5.6 %collective-permute-start.6 = (bf16[128,3072]{1,0:T(8,128)(2,1)S(1)}, bf16[128,3072]{1,0:T(8,128)(2,1)S(1)}, u32[]{:S(2)}, u32[]{:S(2)}) collective-permute-start(bf16[128,3072]{1,0:T(8,128)(2,1)S(1)} %collective-permute-done.2.mine_ref), channel_id=1, source_target_pairs={{0,1},{1,0},{2,3},{3,2},{4,5},{5,4},{6,7},{7,6},{8,9},{9,8},{10,11... | collective-permute-start | bytes 2359304 | tf_op jit(solution)/shard_map/ppermute | solution.py:29
  94.3 1.9 %copy-start.2 = (s32[1,4]{1,0:T(1,128)S(1)}, s32[1,4]{1,0:T(1,128)}, u32[]{:S(2)}) copy-start(s32[1,4]{1,0:T(1,128)} %param.10) | copy-start | bytes 52
  94.4 1.9 %copy-start.3 = (s32[1,4]{1,0:T(1,128)S(1)}, s32[1,4]{1,0:T(1,128)}, u32[]{:S(2)}) copy-start(s32[1,4]{1,0:T(1,128)} %param.11) | copy-start | bytes 52

commit v6 on v5

--- a/solution.py
+++ b/solution.py
@@ -169,8 +169,8 @@
 
 def per_device(traces, offset_bins, class_slots, weights, band_start, smoothing):
     count = traces.shape[0]
-    targets = offset_bins * 2 + class_slots
-    chosen = targets[None, :] == jnp.arange(count, dtype=jnp.int32)[:, None]
+    rank = lax.broadcasted_iota(jnp.int32, (count, count), 0)
+    chosen = (offset_bins[None, :] == rank >> 1) & (class_slots[None, :] == rank & 1)
     ordered = jnp.dot(
         chosen.astype(jnp.bfloat16), traces, preferred_element_type=jnp.float32
     ).astype(jnp.bfloat16)

time: 101 us -> 102 us (level)
  transfers between devices with their start and end apart: 7 -> 7, of which waited for: 3 -> 2; matrix products, arithmetic and copies ran while one was open for 0% -> 0% of each run, Pallas kernels for 4% -> 4%
where the time goes in v6:
time: 102 us
  blocking collectives  53.1 us (52%)
  starting transfers between devices  26.1 us (26%)
  waiting for transfers between devices  11.1 us (11%)
  Pallas kernels  8.2 us (8%)
  local copies, waits for them, and re-layouts  2.31 us (2%)
    all_gather x1, blocking collectives, per_device(): own = lax.all_gather(mine, 'zh', axis=0, tiled=True)  35.7 us
    all_to_all x1, blocking collectives, per_device(): lax.all_to_all(ordered, ('zl', 'y'), split_axis=0, concat_axis=0, tiled=T...  17.4 us
    ppermute x4, starting transfers between devices, swap(): return lax.ppermute(piece, 'c', [(0, 1), (1, 0)])  14.4 us
    ppermute x1, waiting for transfers between devices, per_device(): first, own_other = (forth(own), swap(own))  6.25 us
    ppermute x1, starting transfers between devices, per_device(): far = forth(first)  5.31 us
    ppermute x1, waiting for transfers between devices, per_device(): far = forth(first)  4.8 us
    pallas_call x1, Pallas kernels, per_device(): kernel_call(far_kernel, jax.ShapeDtypeStruct((rows, NT), jnp.bfloat16), [...  4.59 us
    ppermute x1, starting transfers between devices, per_device(): first, own_other = (forth(own), swap(own))  4.4 us
  transfers between devices with their start and end apart: 7, of which 2 were waited for; matrix products, arithmetic and copies ran while one was open for 0% of the time, Pallas kernels for 4%

profile of v6, /device:TPU:1, one launch (start us, length us, event | category | flops | bytes accessed | tf_op | source)
XLA Modules:
  0.0 101.9 jit_solution(4455777075509434679)
XLA Ops:
  0.0 0.0 copy-start
  0.0 0.9 copy-done
  0.9 0.9 convolution_convert_fusion
  1.9 0.1 all_to_all.8
  1.9 17.4 %all_to_all.12 = bf16[16,2,3072]{2,1,0:T(2,128)(2,1)S(1)} all-to-all(bf16[16,2,3072]{2,1,0:T(2,128)(2,1)S(1)} %all_to_all.8), channel_id=1, replica_groups=mesh['zl'=4,'y'=4,'x'=4,'zh'=4,'c'=2] {'zl','y'}, dimensions={0} | all-to-all | bytes 393216 | tf_op jit(solution)/shard_map/all_to_all | solution.py:177
  19.3 0.1 all_to_all.10
  19.4 35.7 %all_gather.3.refs_0_ = bf16[128,3072]{1,0:T(8,128)(2,1)S(1)} all-gather(bf16[32,3072]{1,0:T(8,128)(2,1)S(1)} %all_to_all.10), channel_id=1, replica_groups=mesh['zl'=4,'y'=4,'x'=4,'zh'=4,'c'=2] {'zh'}, dimensions={0}, use_global_device_ids=true | all-gather | bytes 983040 | tf_op jit(solution)/shard_map/all_gather | solution.py:178
  55.1 6.1 %collective-permute-start = (bf16[128,3072]{1,0:T(8,128)(2,1)S(1)}, bf16[128,3072]{1,0:T(8,128)(2,1)S(1)}, u32[]{:S(2)}, u32[]{:S(2)}) collective-permute-start(bf16[128,3072]{1,0:T(8,128)(2,1)S(1)} %all_gather.3.refs_0_), channel_id=1, source_target_pairs={{0,1},{1,0},{2,3},{3,2},{4,5},{5,4},{6,7},{7,6},{8,9},{9,8},{10,11... | collective-permute-start | bytes 2359304 | tf_op jit(solution)/shard_map/ppermute | solution.py:29
  61.2 4.4 %collective-permute-start.1 = (bf16[128,3072]{1,0:T(8,128)(2,1)S(1)}, bf16[128,3072]{1,0:T(8,128)(2,1)S(1)}, u32[]{:S(2)}, u32[]{:S(2)}) collective-permute-start(bf16[128,3072]{1,0:T(8,128)(2,1)S(1)} %all_gather.3.refs_0_), channel_id=1, source_target_pairs={{0,8},{1,25},{8,16},{9,1},{16,24},{17,9},{24,0},{25,17},{2,10},{3,... | collective-permute-start | bytes 2359304 | tf_op jit(solution)/shard_map/ppermute | solution.py:180
  65.6 0.1 pad_add_fusion.where_ref
  65.7 0.0 collective-permute-done.refs_1_
  65.7 0.0 copy-start.1
  65.7 1.2 %copy-done.1 = bf16[1,512,1024]{2,1,0:T(8,128)(2,1)S(1)} copy-done((bf16[1,512,1024]{2,1,0:T(8,128)(2,1)S(1)}, bf16[1,512,1024]{2,1,0:T(8,128)(2,1)}, u32[]{:S(2)}) %copy-start.1) | copy-done | bytes 1048600
  66.9 1.8 %shard_map.64 = (f32[512,3072]{1,0:T(8,128)S(1)}, bf16[512,1024]{1,0:T(8,128)(2,1)S(1)}) custom-call(s32[2]{0:T(128)S(1)} %pad_add_fusion.where_ref, bf16[512,1024]{1,0:T(8,128)(2,1)S(1)} %bitcast.7, bf16[128,3072]{1,0:T(8,128)(2,1)S(1)} %all_gather.3.refs_0_, bf16[128,3072]{1,0:T(8,128)(2,1)S(1)} %collective-permute-done.refs_1_), custom_call_target="tpu_custom_call" | custom-call | flops 3145728 | bytes 256 | tf_op jit(solution)/shard_map/pallas_call | solution.py:185
  68.7 1.9 %collective-permute-start.3 = (bf16[128,3072]{1,0:T(8,128)(2,1)S(1)}, bf16[128,3072]{1,0:T(8,128)(2,1)S(1)}, u32[]{:S(2)}, u32[]{:S(2)}) collective-permute-start(bf16[128,3072]{1,0:T(8,128)(2,1)S(1)} %all_gather.3.refs_0_), channel_id=1, source_target_pairs={{0,24},{1,9},{8,0},{9,17},{16,8},{17,25},{24,16},{25,1},{2,26},{3,... | collective-permute-start | bytes 2359304 | tf_op jit(solution)/shard_map/ppermute | solution.py:192
  70.6 6.2 %collective-permute-done.1.refs_0_ = bf16[128,3072]{1,0:T(8,128)(2,1)S(1)} collective-permute-done((bf16[128,3072]{1,0:T(8,128)(2,1)S(1)}, bf16[128,3072]{1,0:T(8,128)(2,1)S(1)}, u32[]{:S(2)}, u32[]{:S(2)}) %collective-permute-start.1) | collective-permute-done | bytes 786464 | tf_op jit(solution)/shard_map/ppermute | solution.py:180
  76.9 5.3 %collective-permute-start.2 = (bf16[128,3072]{1,0:T(8,128)(2,1)S(1)}, bf16[128,3072]{1,0:T(8,128)(2,1)S(1)}, u32[]{:S(2)}, u32[]{:S(2)}) collective-permute-start(bf16[128,3072]{1,0:T(8,128)(2,1)S(1)} %collective-permute-done.1.refs_0_), channel_id=1, source_target_pairs={{0,8},{1,25},{8,16},{9,1},{16,24},{17,9},{24,0},{25,17},{2,10},{3,... | collective-permute-start | bytes 2359304 | tf_op jit(solution)/shard_map/ppermute | solution.py:194
  82.2 1.9 %collective-permute-start.5 = (bf16[128,3072]{1,0:T(8,128)(2,1)S(1)}, bf16[128,3072]{1,0:T(8,128)(2,1)S(1)}, u32[]{:S(2)}, u32[]{:S(2)}) collective-permute-start(bf16[128,3072]{1,0:T(8,128)(2,1)S(1)} %collective-permute-done.1.refs_0_), channel_id=1, source_target_pairs={{0,1},{1,0},{2,3},{3,2},{4,5},{5,4},{6,7},{7,6},{8,9},{9,8},{10,11... | collective-permute-start | bytes 2359304 | tf_op jit(solution)/shard_map/ppermute | solution.py:29
  84.1 0.0 collective-permute-done.3.refs_2_
  84.1 2.4 %collective-permute-start.4 = (bf16[128,3072]{1,0:T(8,128)(2,1)S(1)}, bf16[128,3072]{1,0:T(8,128)(2,1)S(1)}, u32[]{:S(2)}, u32[]{:S(2)}) collective-permute-start(bf16[128,3072]{1,0:T(8,128)(2,1)S(1)} %collective-permute-done.3.refs_2_), channel_id=1, source_target_pairs={{0,1},{1,0},{2,3},{3,2},{4,5},{5,4},{6,7},{7,6},{8,9},{9,8},{10,11... | collective-permute-start | bytes 2359304 | tf_op jit(solution)/shard_map/ppermute | solution.py:29
  86.5 4.8 %collective-permute-done.2.mine_ref = bf16[128,3072]{1,0:T(8,128)(2,1)S(1)} collective-permute-done((bf16[128,3072]{1,0:T(8,128)(2,1)S(1)}, bf16[128,3072]{1,0:T(8,128)(2,1)S(1)}, u32[]{:S(2)}, u32[]{:S(2)}) %collective-permute-start.2) | collective-permute-done | bytes 786464 | tf_op jit(solution)/shard_map/ppermute | solution.py:194
  91.3 4.0 %collective-permute-start.6 = (bf16[128,3072]{1,0:T(8,128)(2,1)S(1)}, bf16[128,3072]{1,0:T(8,128)(2,1)S(1)}, u32[]{:S(2)}, u32[]{:S(2)}) collective-permute-start(bf16[128,3072]{1,0:T(8,128)(2,1)S(1)} %collective-permute-done.2.mine_ref), channel_id=1, source_target_pairs={{0,1},{1,0},{2,3},{3,2},{4,5},{5,4},{6,7},{7,6},{8,9},{9,8},{10,11... | collective-permute-start | bytes 2359304 | tf_op jit(solution)/shard_map/ppermute | solution.py:29
  95.4 0.0 collective-permute-done.5.refs_3_
  95.4 0.0 collective-permute-done.4.refs_1_
  95.4 0.0 copy-start.2
  95.4 0.0 copy-start.3
  95.4 1.8 %shard_map.65.near_ref = f32[512,3072]{1,0:T(8,128)S(1)} custom-call(bf16[512,1024]{1,0:T(8,128)(2,1)S(1)} %get-tuple-element.13.weights_ref, f32[512,3072]{1,0:T(8,128)S(1)} %get-tuple-element.18.product_ref, bf16[128,3072]{1,0:T(8,128)(2,1)S(1)} %collective-permute-done.1.refs_0_, bf16[128,3072]{1,0:T(8,128)(2,1)S(1)} %collective-permute-done.4.refs_1_, ...), custom_call_target="tpu_custom_call" | custom-call | flops 6291456 | bytes 512 | tf_op jit(solution)/shard_map/pallas_call | solution.py:197
  97.2 0.0 collective-permute-done.6.theirs_ref
  97.3 0.0 copy-done.2
  97.3 0.0 copy-done.3
  97.3 4.6 %shard_map.66 = bf16[512,1536]{1,0:T(8,128)(2,1)} custom-call(s32[4]{0:T(128)S(1)} %bitcast.8, s32[4]{0:T(128)S(1)} %bitcast.9, bf16[512,1024]{1,0:T(8,128)(2,1)S(1)} %get-tuple-element.13.weights_ref, f32[512,3072]{1,0:T(8,128)S(1)} %shard_map.65.near_ref, bf16[128,3072]{1,0:T(8,128)(2,1)S(1)} %collective-permute-done.2.mine_ref, ...), custom_call_target="tpu_custom_call" | custom-call | flops 3145728 | bytes 256 | tf_op jit(solution)/shard_map/pallas_call | solution.py:198
  (1 shorter events, 0.0 us)
Async XLA Ops:
  0.0 0.9 copy-start
  55.1 10.6 %collective-permute-start = (bf16[128,3072]{1,0:T(8,128)(2,1)S(1)}, bf16[128,3072]{1,0:T(8,128)(2,1)S(1)}, u32[]{:S(2)}, u32[]{:S(2)}) collective-permute-start(bf16[128,3072]{1,0:T(8,128)(2,1)S(1)} %all_gather.3.refs_0_), channel_id=1, source_target_pairs={{0,1},{1,0},{2,3},{3,2},{4,5},{5,4},{6,7},{7,6},{8,9},{9,8},{10,11... | collective-permute-start | bytes 2359304 | tf_op jit(solution)/shard_map/ppermute | solution.py:29
  61.2 15.7 %collective-permute-start.1 = (bf16[128,3072]{1,0:T(8,128)(2,1)S(1)}, bf16[128,3072]{1,0:T(8,128)(2,1)S(1)}, u32[]{:S(2)}, u32[]{:S(2)}) collective-permute-start(bf16[128,3072]{1,0:T(8,128)(2,1)S(1)} %all_gather.3.refs_0_), channel_id=1, source_target_pairs={{0,8},{1,25},{8,16},{9,1},{16,24},{17,9},{24,0},{25,17},{2,10},{3,... | collective-permute-start | bytes 2359304 | tf_op jit(solution)/shard_map/ppermute | solution.py:180
  65.7 1.2 %copy-start.1 = (bf16[1,512,1024]{2,1,0:T(8,128)(2,1)S(1)}, bf16[1,512,1024]{2,1,0:T(8,128)(2,1)}, u32[]{:S(2)}) copy-start(bf16[1,512,1024]{2,1,0:T(8,128)(2,1)} %param.9) | copy-start | bytes 3145732
  68.7 15.4 %collective-permute-start.3 = (bf16[128,3072]{1,0:T(8,128)(2,1)S(1)}, bf16[128,3072]{1,0:T(8,128)(2,1)S(1)}, u32[]{:S(2)}, u32[]{:S(2)}) collective-permute-start(bf16[128,3072]{1,0:T(8,128)(2,1)S(1)} %all_gather.3.refs_0_), channel_id=1, source_target_pairs={{0,24},{1,9},{8,0},{9,17},{16,8},{17,25},{24,16},{25,1},{2,26},{3,... | collective-permute-start | bytes 2359304 | tf_op jit(solution)/shard_map/ppermute | solution.py:192
  76.9 14.5 %collective-permute-start.2 = (bf16[128,3072]{1,0:T(8,128)(2,1)S(1)}, bf16[128,3072]{1,0:T(8,128)(2,1)S(1)}, u32[]{:S(2)}, u32[]{:S(2)}) collective-permute-start(bf16[128,3072]{1,0:T(8,128)(2,1)S(1)} %collective-permute-done.1.refs_0_), channel_id=1, source_target_pairs={{0,8},{1,25},{8,16},{9,1},{16,24},{17,9},{24,0},{25,17},{2,10},{3,... | collective-permute-start | bytes 2359304 | tf_op jit(solution)/shard_map/ppermute | solution.py:194
  82.2 13.2 %collective-permute-start.5 = (bf16[128,3072]{1,0:T(8,128)(2,1)S(1)}, bf16[128,3072]{1,0:T(8,128)(2,1)S(1)}, u32[]{:S(2)}, u32[]{:S(2)}) collective-permute-start(bf16[128,3072]{1,0:T(8,128)(2,1)S(1)} %collective-permute-done.1.refs_0_), channel_id=1, source_target_pairs={{0,1},{1,0},{2,3},{3,2},{4,5},{5,4},{6,7},{7,6},{8,9},{9,8},{10,11... | collective-permute-start | bytes 2359304 | tf_op jit(solution)/shard_map/ppermute | solution.py:29
  84.1 11.3 %collective-permute-start.4 = (bf16[128,3072]{1,0:T(8,128)(2,1)S(1)}, bf16[128,3072]{1,0:T(8,128)(2,1)S(1)}, u32[]{:S(2)}, u32[]{:S(2)}) collective-permute-start(bf16[128,3072]{1,0:T(8,128)(2,1)S(1)} %collective-permute-done.3.refs_2_), channel_id=1, source_target_pairs={{0,1},{1,0},{2,3},{3,2},{4,5},{5,4},{6,7},{7,6},{8,9},{9,8},{10,11... | collective-permute-start | bytes 2359304 | tf_op jit(solution)/shard_map/ppermute | solution.py:29
  91.3 5.9 %collective-permute-start.6 = (bf16[128,3072]{1,0:T(8,128)(2,1)S(1)}, bf16[128,3072]{1,0:T(8,128)(2,1)S(1)}, u32[]{:S(2)}, u32[]{:S(2)}) collective-permute-start(bf16[128,3072]{1,0:T(8,128)(2,1)S(1)} %collective-permute-done.2.mine_ref), channel_id=1, source_target_pairs={{0,1},{1,0},{2,3},{3,2},{4,5},{5,4},{6,7},{7,6},{8,9},{9,8},{10,11... | collective-permute-start | bytes 2359304 | tf_op jit(solution)/shard_map/ppermute | solution.py:29
  95.4 1.9 %copy-start.2 = (s32[1,4]{1,0:T(1,128)S(1)}, s32[1,4]{1,0:T(1,128)}, u32[]{:S(2)}) copy-start(s32[1,4]{1,0:T(1,128)} %param.10) | copy-start | bytes 52
  95.4 1.9 %copy-start.3 = (s32[1,4]{1,0:T(1,128)S(1)}, s32[1,4]{1,0:T(1,128)}, u32[]{:S(2)}) copy-start(s32[1,4]{1,0:T(1,128)} %param.11) | copy-start | bytes 52
